TPU v7x, 32 devices: a whole 2x2x4 slice. The times are simulated.
32 devices in a mesh: cuts: 2 (over x), region: 16 (over z, y, core).
Axes of the slice: x: 2, y: 2, z: 4, core: 2. Of those that a mesh axis runs over, the one named last changes fastest.
Arguments:
- objects: float32 [2, 2, 4096, 1024], P('cuts', None, 'region'), may hold values from -4 to 4
- probes: bfloat16 [4, 2, 256, 256], replicated, may hold values from -4 to 4
- amplitudes: float32 [64, 256, 256], P('region'), may hold values from 0.2 to 2.5
- prop_phase: float32 [256, 256], replicated, may hold values from -3.140625 to 3.140625
- scan_rows: int32 [64], P('region'), may hold values from -128 to 128, as said below
- scan_cols: int32 [64], P('region'), may hold values from 0 to 768
- probe_choice: int32 [64], P('region'), may hold values from 0 to 3
Outputs:
- gradient: float32 [2, 2, 4096, 1024], P('cuts', None, 'region')
Inputs may be any that keep to these rules, and one draw needn't show every extreme that they name: `scan_rows`: in every region, half of the positions start between 64 and 128 rows above the band's first row, and the other half end between 64 and 128 rows below its last row.
All inputs are finite; a program needn't handle non-finite values.
Results may differ from a plain program's by a relative error of at most 0.039.
Values may be sent and summed in bfloat16 or wider, within the bound.
A program may use at most 64 MiB of HBM per device.

v0:
```python
import functools
import jax
import jax.numpy as jnp
import numpy as np
from jax import lax
from jax.experimental import pallas as pl
from jax.experimental.pallas import tpu as pltpu
from jax.sharding import PartitionSpec as P

modulus_floor = 0.25
LANES = 128
SUBLANES = 8
VMEM = pl.BlockSpec(memory_space=pltpu.VMEM)
SMEM = pl.BlockSpec(memory_space=pltpu.SMEM)
LIMIT = pltpu.CompilerParams(vmem_limit_bytes=60000 * 1024)


def dft_blocks(side):
    indices = np.arange(side)
    angles = (indices[:, None] * indices[None, :] % side) * (2.0 * np.pi / side)
    real = np.cos(angles) / np.sqrt(side)
    imag = np.sin(angles) / np.sqrt(side)
    tables = []
    for sign in (-1.0, 1.0):
        tables.append(np.block([[real, -sign * imag], [sign * imag, real]]))
        tables.append(np.block([[real, sign * imag], [-sign * imag, real]]))
    return jnp.asarray(np.stack(tables), dtype=jnp.bfloat16)


def split_col(col, cols, side):
    base = jnp.minimum(lax.div(col, LANES), (cols - side) // LANES - 1) * LANES
    return base, col - base


def cut_window(ext, plane, row, col, height, side):
    base, shift = split_col(col, ext.shape[2], side)
    top = lax.div(row, SUBLANES) * SUBLANES
    tall = height + SUBLANES
    block = ext[plane, pl.ds(top, tall), pl.ds(base, side + LANES)]
    block = pltpu.roll(block, lax.rem(tall + top - row, tall), axis=0)[:height]
    back = lax.rem(LANES - shift + LANES, LANES)
    chunks = [
        pltpu.roll(block[:, j : j + LANES], back, axis=1) for j in range(0, side + LANES, LANES)
    ]
    lane = lax.broadcasted_iota(jnp.int32, (height, LANES), 1)
    keep = lane < LANES - shift
    return jnp.concatenate(
        [jnp.where(keep, chunks[j], chunks[j + 1]) for j in range(len(chunks) - 1)], axis=1
    )


def add_window(grad, plane, row, col, field):
    height, side = field.shape
    base, shift = split_col(col, grad.shape[2], side)
    top = lax.div(row, SUBLANES) * SUBLANES
    tall = height + SUBLANES
    field = jnp.concatenate([field, jnp.zeros((SUBLANES, side), field.dtype)], axis=0)
    field = pltpu.roll(field, row - top, axis=0)
    ahead = lax.rem(shift, LANES)
    chunks = [pltpu.roll(field[:, j : j + LANES], ahead, axis=1) for j in range(0, side, LANES)]
    lane = lax.broadcasted_iota(jnp.int32, (tall, LANES), 1)
    keep = lane >= shift
    zero = jnp.zeros((tall, LANES), field.dtype)
    parts = [zero] + chunks + [zero]
    placed = jnp.concatenate(
        [jnp.where(keep, parts[j + 1], parts[j]) for j in range(len(chunks) + 1)], axis=1
    )
    where = (plane, pl.ds(top, tall), pl.ds(base, side + LANES))
    grad[where] = grad[where] + placed


def dot(left, right):
    return jnp.dot(left, right, preferred_element_type=jnp.float32)


def transform(field, tables, which):
    side = field[0].shape[0]
    stacked = jnp.concatenate([field[0].astype(jnp.bfloat16), field[1].astype(jnp.bfloat16)], axis=0)
    middle = dot(tables[which], stacked).astype(jnp.bfloat16)
    beside = jnp.concatenate([middle[:side], middle[side:]], axis=1)
    result = dot(beside, tables[which + 1])
    return result[:, :side], result[:, side:]


def multiply(left, right):
    return left[0] * right[0] - left[1] * right[1], left[0] * right[1] + left[1] * right[0]


def multiply_conjugate(left, right):
    return left[0] * right[0] + left[1] * right[1], left[0] * right[1] - left[1] * right[0]


def narrowed(field):
    return tuple(part.astype(jnp.bfloat16).astype(jnp.float32) for part in field)


def one_position(psi0, object0, object1, measured, wave, tables):
    psi1 = narrowed(
        transform(multiply(wave, transform(multiply(psi0, object0), tables, 0)), tables, 2)
    )
    far = transform(multiply(psi1, object1), tables, 0)
    modulus = jnp.sqrt(far[0] * far[0] + far[1] * far[1])
    factor = 1.0 - measured / jnp.maximum(modulus, modulus_floor)
    g1 = narrowed(transform((far[0] * factor, far[1] * factor), tables, 2))
    d1 = multiply_conjugate(psi1, g1)
    back = transform(multiply_conjugate(object1, g1), tables, 0)
    g0 = narrowed(transform(multiply_conjugate(wave, back), tables, 2))
    return multiply_conjugate(psi0, g0), d1


def wide(ref, *index):
    return ref[index + (0,)].astype(jnp.float32), ref[index + (1,)].astype(jnp.float32)


def pick(info, kind, side_index, rank, values):
    seen = jnp.int32(0)
    chosen = jnp.int32(0)
    for position in range(info[0].shape[0]):
        above = info[0][position] < 0
        here = above if side_index == 0 else jnp.logical_not(above)
        match = jnp.logical_and(here, seen == rank)
        chosen = chosen + jnp.where(match, values(position), 0)
        seen = seen + jnp.where(here, 1, 0)
    return chosen


def corner(info, side_index, rank):
    row = pick(info, 0, side_index, rank, lambda position: info[0][position])
    col = pick(info, 1, side_index, rank, lambda position: info[1][position])
    return row, col


def near_rows(side_index, side):
    return (side // 4, side) if side_index == 0 else (0, side - side // 4)


def far_rows(side_index, side):
    return (0, side // 2) if side_index == 0 else (side // 2, side)


def wave_kernel(
    side, count, scans, choice_any, band, probes_any, amps_any, phase_any, tables_any,
    mine, near_out, far_out, around,
    ext, probes, amps, phase, wave, tables,
    near_send, far_send, near_in, far_in, near_back, far_back, here, before, after, choice,
    local_sem, info_sem, send_sem, recv_sem,
):
    rim = side // 2
    quarter = side // 4
    band_rows = band.shape[1]
    c = lax.axis_index("cuts")
    region = lax.axis_index("region")
    other_cut = 1 - c
    prior = lax.rem(region + count - 1, count)
    following = lax.rem(region + 1, count)
    loads = [
        pltpu.make_async_copy(source, target, local_sem.at[k])
        for k, (source, target) in enumerate((
            (scans[0], here[0]), (scans[1], here[1]), (choice_any, choice),
            (band, ext.at[:, pl.ds(rim, band_rows)]), (phase_any, phase),
            (tables_any, tables), (probes_any, probes), (amps_any, amps),
        ))
    ]
    for load in loads:
        load.start()
    barrier = pltpu.get_barrier_semaphore()
    peers = [(other_cut, region)]
    peers += [(q, t) for q in (c, other_cut) for t in (prior, following)]
    for peer in peers:
        pl.semaphore_signal(barrier, 1, device_id=peer, device_id_type=pl.DeviceIdType.MESH)
    pl.semaphore_wait(barrier, len(peers))

    def remote(source, target, slot, peer):
        return pltpu.make_async_remote_copy(
            src_ref=source, dst_ref=target,
            send_sem=send_sem.at[slot], recv_sem=recv_sem.at[slot],
            device_id=peer, device_id_type=pl.DeviceIdType.MESH,
        )

    notes = []
    for k, (source, target) in enumerate(zip(scans + scans, around)):
        notes.append(remote(source, target, 12 + k, (c, following if k < 2 else prior)))
        notes[-1].start()
    for load in loads[:4]:
        load.wait()
    sends = [[], []]
    for d in range(2):
        row, col = corner(here, d, other_cut)
        low, high = near_rows(d, side)
        for plane in range(2):
            near_send[d, plane] = cut_window(
                ext, plane, row + rim + low, col, high - low, side
            ).astype(jnp.bfloat16)
        sends[d].append(remote(near_send.at[d], near_in.at[d], 6 * d, (other_cut, region)))
        sends[d][0].start()
        if d == 0:
            fetches = []
            for k, target in enumerate(before + after):
                notes[k].wait()
                fetches.append(pltpu.make_async_copy(around[k], target, info_sem.at[k]))
                fetches[-1].start()
            for fetch in fetches:
                fetch.wait()
        info, peer_region, offset = (
            (after, following, band_rows) if d == 0 else (before, prior, -band_rows)
        )
        low, high = far_rows(d, side)
        for j, q in enumerate((c, other_cut)):
            row, col = corner(info, d, q)
            for plane in range(2):
                far_send[d, j, plane] = cut_window(
                    ext, plane, row + rim + offset + low, col, high - low, side
                ).astype(jnp.bfloat16)
            copy = remote(far_send.at[d, j], far_in.at[d, j], 6 * d + 1 + j, (q, peer_region))
            copy.start()
            sends[d].append(copy)
    for load in loads[4:]:
        load.wait()
    wave[0] = jnp.cos(phase[...])
    wave[1] = jnp.sin(phase[...])
    first = c == 0
    backs = []
    ids = lax.broadcasted_iota(jnp.int32, (rim, side), 0)
    for d in range(2):
        position = pick(here, 0, d, c, lambda p: p)
        chosen = pick(here, 0, d, c, lambda p: choice[p])
        row, col = corner(here, d, c)
        psi0 = wide(probes, chosen)
        own = [cut_window(ext, plane, row + rim, col, side, side) for plane in range(2)]
        for copy in sends[d]:
            copy.wait_recv()
        other = []
        for plane in range(2):
            far = far_in[d, 0, plane].astype(jnp.float32)
            far_other = far_in[d, 1, plane].astype(jnp.float32)
            near_other = near_in[d, plane].astype(jnp.float32)
            near_own = own[plane]
            if d == 0:
                mixed = jnp.where(ids < -row, far, near_own[:rim])
                own[plane] = jnp.concatenate([mixed, near_own[rim:]], axis=0)
                mixed = jnp.where(ids[quarter:] < -row, far_other[quarter:], near_other[:quarter])
                parts = [far_other[:quarter], mixed, near_other[quarter:]]
            else:
                mixed = jnp.where(ids >= rim - row, far, near_own[rim:])
                own[plane] = jnp.concatenate([near_own[:rim], mixed], axis=0)
                mixed = jnp.where(ids[:quarter] >= rim - row, far_other[:quarter], near_other[rim:])
                parts = [near_other[:rim], mixed, far_other[quarter:]]
            other.append(jnp.concatenate(parts, axis=0))
        object0 = tuple(jnp.where(first, x, y) for x, y in zip(own, other))
        object1 = tuple(jnp.where(first, y, x) for x, y in zip(own, other))
        d0, d1 = one_position(psi0, object0, object1, amps[position], (wave[0], wave[1]), tables)
        peer_region = prior if d == 0 else following
        near_low, near_high = near_rows(d, side)
        low, high = far_rows(d, side)
        for plane in range(2):
            kept = jnp.where(first, d0[plane], d1[plane]).astype(jnp.bfloat16)
            given = jnp.where(first, d1[plane], d0[plane]).astype(jnp.bfloat16)
            mine[d, plane] = kept[near_low:near_high]
            near_back[d, plane] = given[near_low:near_high]
            far_back[d, 0, plane] = kept[low:high]
            far_back[d, 1, plane] = given[low:high]
        backs.append(remote(near_back.at[d], near_out.at[d], 6 * d + 3, (other_cut, region)))
        for j, q in enumerate((c, other_cut)):
            backs.append(
                remote(far_back.at[d, j], far_out.at[d, j], 6 * d + 4 + j, (q, peer_region))
            )
        for copy in backs[-3:]:
            copy.start()
    for copy in sends[0] + sends[1]:
        copy.wait_send()
    for copy in backs:
        copy.wait()


def deposit_kernel(
    side, scans, around, mine, near, far, out, grad, here, before, after, local_sem, out_sem
):
    rim = side // 2
    band_rows = out.shape[1]
    c = lax.axis_index("cuts")
    loads = [
        pltpu.make_async_copy(source, target, local_sem.at[k])
        for k, (source, target) in enumerate(zip(scans + around, here + before + after))
    ]
    for load in loads:
        load.start()
    grad[...] = jnp.zeros_like(grad)
    for load in loads:
        load.wait()
    stores = []
    for plane in range(2):
        for d in range(2):
            low, _ = near_rows(d, side)
            far_low, _ = far_rows(d, side)
            info, offset = (after, band_rows) if d == 0 else (before, -band_rows)
            parts = [
                (mine.at[d], here, c, rim + low),
                (near.at[d], here, 1 - c, rim + low),
                (far.at[d, 0], info, c, rim + offset + far_low),
                (far.at[d, 1], info, 1 - c, rim + offset + far_low),
            ]
            for source, table, rank, shift in parts:
                row, col = corner(table, d, rank)
                add_window(grad, plane, row + shift, col, source[plane].astype(jnp.float32))
        stores.append(
            pltpu.make_async_copy(
                grad.at[plane, pl.ds(rim, band_rows)], out.at[plane], out_sem.at[plane]
            )
        )
        stores[-1].start()
    for store in stores:
        store.wait()


def shards(objects, probes, amplitudes, prop_phase, scan_rows, scan_cols, probe_choice):
    side = probes.shape[-1]
    rim = side // 2
    count = lax.axis_size("region")
    band = objects[0]
    band_rows, columns = band.shape[1:]
    tables = dft_blocks(side)
    near = (2, 2, side - side // 4, side)
    far = (2, 2, 2, rim, side)
    held = lambda shape: jax.ShapeDtypeStruct(shape, jnp.bfloat16)
    slot = lambda shape: pltpu.VMEM(shape, jnp.bfloat16)
    tall = pltpu.VMEM((2, band_rows + 2 * rim + SUBLANES, columns), jnp.float32)
    ANY = pl.BlockSpec(memory_space=pl.ANY)
    scans = (scan_rows, scan_cols)
    info = jax.ShapeDtypeStruct(scan_rows.shape, jnp.int32)
    scalars = pltpu.SMEM(scan_rows.shape, jnp.int32)
    mine, near_part, far_part, around = pl.pallas_call(
        functools.partial(wave_kernel, side, count),
        out_shape=(held(near), held(near), held(far), (info,) * 4),
        in_specs=[(ANY, ANY)] + [ANY] * 6,
        out_specs=(VMEM, VMEM, VMEM, (ANY,) * 4),
        scratch_shapes=[
            tall,
            pltpu.VMEM(probes.shape, probes.dtype),
            pltpu.VMEM(amplitudes.shape, amplitudes.dtype),
            pltpu.VMEM(prop_phase.shape, jnp.float32),
            pltpu.VMEM((2,) + prop_phase.shape, jnp.float32),
            pltpu.VMEM(tables.shape, tables.dtype),
            slot(near), slot(far), slot(near), slot(far), slot(near), slot(far),
            (scalars,) * 2, (scalars,) * 2, (scalars,) * 2, scalars,
            pltpu.SemaphoreType.DMA((8,)),
            pltpu.SemaphoreType.DMA((4,)),
            pltpu.SemaphoreType.DMA((16,)),
            pltpu.SemaphoreType.DMA((16,)),
        ],
        compiler_params=pltpu.CompilerParams(
            collective_id=0, has_side_effects=True, vmem_limit_bytes=60000 * 1024
        ),
    )(scans, probe_choice, band, probes, amplitudes, prop_phase, tables)
    out = pl.pallas_call(
        functools.partial(deposit_kernel, side),
        out_shape=jax.ShapeDtypeStruct(band.shape, jnp.float32),
        in_specs=[(ANY, ANY), (ANY,) * 4] + [VMEM] * 3,
        out_specs=ANY,
        scratch_shapes=[
            tall, (scalars,) * 2, (scalars,) * 2, (scalars,) * 2,
            pltpu.SemaphoreType.DMA((6,)),
            pltpu.SemaphoreType.DMA((2,)),
        ],
        compiler_params=LIMIT,
    )(scans, around, mine, near_part, far_part)
    return out[None]


def solution(mesh):
    return jax.shard_map(
        shards,
        mesh=mesh,
        in_specs=(
            P("cuts", None, "region", None),
            P(),
            P("region", None, None),
            P(),
            P("region"),
            P("region"),
            P("region"),
        ),
        out_specs=P("cuts", None, "region", None),
        check_vma=False,
    )
```

profile of v0, /device:TPU:1, one launch (start us, length us, event | category | flops | bytes accessed | tf_op | source)
XLA Modules:
  0.0 41.1 jit_solution(11491069013671849660)
XLA Ops:
  0.0 36.8 %shard_map.82 = (bf16[2,2,192,256]{3,2,1,0:T(8,128)(2,1)}, bf16[2,2,192,256]{3,2,1,0:T(8,128)(2,1)}, bf16[2,2,2,128,256]{4,3,2,1,0:T(8,128)(2,1)}, s32[4]{0:T(12...) custom-call(s32[4]{0:T(128)} %scans_0_.3, s32[4]{0:T(128)} %scans_1_.3, s32[4]{0:T(128)} %choice_any.1, ...), custom_call_target="tpu_custom_call" | custom-call | tf_op jit(solution)/shard_map/pallas_call | solution.py:331
  36.8 4.3 %shard_map.83 = f32[2,256,1024]{2,1,0:T(8,128)} custom-call(s32[4]{0:T(128)} %scans_0_.3, s32[4]{0:T(128)} %scans_1_.3, s32[4]{0:T(128)} %get-tuple-element.12.around_0_, s32[4]{0:T(128)} %get-tuple-element.13.around_1_, s32[4]{0:T(128)} %get-tuple-element.14.around_2_, s32[4]{0:T(128)} %get-tuple-element.15.around_3_, ...), custom_call_target="tpu_custom_call" | custom-call | tf_op jit(solution)/shard_map/pallas_call | solution.py:354
where the time goes:
time: 41.3 us; the launch traced here: 41.1 us
  Pallas kernels  41.1 us (100%)
    pallas_call x1, Pallas kernels, shards(): pl.pallas_call(functools.partial(wave_kernel, side, count), out_shape=(he...  36.8 us
    pallas_call x1, Pallas kernels, shards(): pl.pallas_call(functools.partial(deposit_kernel, side), out_shape=jax.Sha...  4.32 us

commit v1 on v0

v1 whole, which is shorter than its diff:
```python
import functools
import jax
import jax.numpy as jnp
import numpy as np
from jax import lax
from jax.experimental import pallas as pl
from jax.experimental.pallas import tpu as pltpu
from jax.sharding import PartitionSpec as P

modulus_floor = 0.25
LANES = 128
SUBLANES = 8
VMEM = pl.BlockSpec(memory_space=pltpu.VMEM)
SMEM = pl.BlockSpec(memory_space=pltpu.SMEM)
LIMIT = pltpu.CompilerParams(vmem_limit_bytes=60000 * 1024)


def dft_blocks(side):
    indices = np.arange(side)
    angles = (indices[:, None] * indices[None, :] % side) * (2.0 * np.pi / side)
    real = np.cos(angles) / np.sqrt(side)
    imag = np.sin(angles) / np.sqrt(side)
    tables = [np.block([[real, imag], [-imag, real]]), np.block([[real, -imag], [imag, real]])]
    return jnp.asarray(np.stack(tables), dtype=jnp.bfloat16)


def split_col(col, cols, side):
    base = jnp.minimum(lax.div(col, LANES), (cols - side) // LANES - 1) * LANES
    return base, col - base


def cut_window(ext, plane, row, col, height, side):
    base, shift = split_col(col, ext.shape[2], side)
    top = lax.div(row, SUBLANES) * SUBLANES
    tall = height + SUBLANES
    block = ext[plane, pl.ds(top, tall), pl.ds(base, side + LANES)]
    block = pltpu.roll(block, lax.rem(tall + top - row, tall), axis=0)[:height]
    back = lax.rem(LANES - shift + LANES, LANES)
    chunks = [
        pltpu.roll(block[:, j : j + LANES], back, axis=1) for j in range(0, side + LANES, LANES)
    ]
    lane = lax.broadcasted_iota(jnp.int32, (height, LANES), 1)
    keep = lane < LANES - shift
    return jnp.concatenate(
        [jnp.where(keep, chunks[j], chunks[j + 1]) for j in range(len(chunks) - 1)], axis=1
    )


def add_window(grad, plane, row, col, field):
    height, side = field.shape
    base, shift = split_col(col, grad.shape[2], side)
    top = lax.div(row, SUBLANES) * SUBLANES
    tall = height + SUBLANES
    field = jnp.concatenate([field, jnp.zeros((SUBLANES, side), field.dtype)], axis=0)
    field = pltpu.roll(field, row - top, axis=0)
    ahead = lax.rem(shift, LANES)
    chunks = [pltpu.roll(field[:, j : j + LANES], ahead, axis=1) for j in range(0, side, LANES)]
    lane = lax.broadcasted_iota(jnp.int32, (tall, LANES), 1)
    keep = lane >= shift
    zero = jnp.zeros((tall, LANES), field.dtype)
    parts = [zero] + chunks + [zero]
    placed = jnp.concatenate(
        [jnp.where(keep, parts[j + 1], parts[j]) for j in range(len(chunks) + 1)], axis=1
    )
    where = (plane, pl.ds(top, tall), pl.ds(base, side + LANES))
    grad[where] = grad[where] + placed


def dot(left, right):
    return jnp.dot(left, right, preferred_element_type=jnp.float32)


def transform(field, tables, which):
    side = field[0].shape[0]
    stacked = jnp.concatenate([field[0].astype(jnp.bfloat16), field[1].astype(jnp.bfloat16)], axis=0)
    middle = dot(tables[which], stacked).astype(jnp.bfloat16)
    beside = jnp.concatenate([middle[:side], middle[side:]], axis=1)
    result = dot(beside, tables[1 - which])
    return result[:, :side], result[:, side:]


def multiply(left, right):
    return left[0] * right[0] - left[1] * right[1], left[0] * right[1] + left[1] * right[0]


def multiply_conjugate(left, right):
    return left[0] * right[0] + left[1] * right[1], left[0] * right[1] - left[1] * right[0]


def narrowed(field):
    return tuple(part.astype(jnp.bfloat16).astype(jnp.float32) for part in field)


def one_position(psi0, object0, object1, measured, wave, tables):
    psi1 = narrowed(
        transform(multiply(wave, transform(multiply(psi0, object0), tables, 0)), tables, 1)
    )
    far = transform(multiply(psi1, object1), tables, 0)
    modulus = jnp.sqrt(far[0] * far[0] + far[1] * far[1])
    factor = 1.0 - measured / jnp.maximum(modulus, modulus_floor)
    g1 = narrowed(transform((far[0] * factor, far[1] * factor), tables, 1))
    d1 = multiply_conjugate(psi1, g1)
    back = transform(multiply_conjugate(object1, g1), tables, 0)
    g0 = narrowed(transform(multiply_conjugate(wave, back), tables, 1))
    return multiply_conjugate(psi0, g0), d1


def wide(ref, *index):
    return ref[index + (0,)].astype(jnp.float32), ref[index + (1,)].astype(jnp.float32)


def find(rows, upper, rank):
    seen = jnp.int32(0)
    chosen = jnp.int32(0)
    for position in range(rows.shape[0]):
        here = jnp.where(rows[position] < 0, 1, 0) == upper
        chosen = jnp.where(jnp.logical_and(here, seen == rank), position, chosen)
        seen = seen + jnp.where(here, 1, 0)
    return chosen


def corner(info, upper, rank):
    position = find(info[0], upper, rank)
    return info[0][position], info[1][position]


class Step:
    def __init__(self, index, region, count, side, band_rows):
        self.index = index
        even = 1 - lax.rem(region, 2)
        self.upper = 1 - even if index == 0 else even
        before = lax.rem(region + count - 1, count)
        after = lax.rem(region + 1, count)
        self.peer = jnp.where(self.upper == 1, before, after)
        half = side // 2
        self.near_low = pl.multiple_of(self.upper * half, half)
        self.far_low = pl.multiple_of((1 - self.upper) * half, half)
        self.peer_upper = 1 - self.upper
        self.peer_offset = (2 * self.peer_upper - 1) * band_rows
        self.peer_far_low = self.near_low
        self.wraps = jnp.logical_and(self.upper == 1, region == 0) | jnp.logical_and(
            self.upper == 0, region == count - 1
        )


def wave_kernel(
    side, count, scans, choice_any, band, probes_any, amps_any, phase_any, tables_any,
    coords, keep, give_in, far_back,
    ext, probes, amps, phase, wave, tables,
    x_send, x_in, far_send, far_in, own, give,
    here, around, choice,
    local_sem, send_sem, recv_sem,
):
    rim = side // 2
    band_rows = band.shape[1]
    c = lax.axis_index("cuts")
    region = lax.axis_index("region")
    other_cut = 1 - c
    steps = [Step(s, region, count, side, band_rows) for s in range(2)]
    loads = [
        pltpu.make_async_copy(source, target, local_sem.at[k])
        for k, (source, target) in enumerate((
            (scans[0], here[0]), (scans[1], here[1]),
            (band, ext.at[:, pl.ds(rim, band_rows)]), (choice_any, choice), (phase_any, phase),
            (tables_any, tables), (probes_any, probes), (amps_any, amps),
        ))
    ]
    for load in loads:
        load.start()
    barrier = pltpu.get_barrier_semaphore()
    peers = [(other_cut, region)] + [(c, step.peer) for step in steps]
    for peer in peers:
        pl.semaphore_signal(barrier, 1, device_id=peer, device_id_type=pl.DeviceIdType.MESH)
    pl.semaphore_wait(barrier, len(peers))
    slots = iter(range(24))

    def remote(source, target, peer):
        slot = next(slots)
        return pltpu.make_async_remote_copy(
            src_ref=source, dst_ref=target,
            send_sem=send_sem.at[slot], recv_sem=recv_sem.at[slot],
            device_id=peer, device_id_type=pl.DeviceIdType.MESH,
        )

    across = (other_cut, region)
    notes = [
        [remote(scans[k], around[s][k], (c, steps[s].peer)) for k in range(2)] for s in range(2)
    ]
    near = [pl.ds(step.near_low, rim) for step in steps]
    far = [pl.ds(step.far_low, rim) for step in steps]
    x_near = [remote(x_send.at[s, :, near[s]], x_in.at[s, :, near[s]], across) for s in range(2)]
    x_far = [remote(x_send.at[s, :, far[s]], x_in.at[s, :, far[s]], across) for s in range(2)]
    halo = [
        [remote(far_send.at[s, j], far_in.at[s, j], (c, steps[s].peer)) for j in range(2)]
        for s in range(2)
    ]
    give_far = [remote(give.at[s, :, far[s]], give_in.at[s, :, far[s]], across) for s in range(2)]
    give_near = [remote(give.at[s, :, near[s]], give_in.at[s, :, near[s]], across) for s in range(2)]
    back_own = [
        remote(keep.at[s, :, far[s]], far_back.at[s, 0], (c, steps[s].peer)) for s in range(2)
    ]
    back_other = [
        remote(give_in.at[s, :, far[s]], far_back.at[s, 1], (c, steps[s].peer)) for s in range(2)
    ]
    for pair in notes:
        for note in pair:
            note.start()
    for load in loads[:3]:
        load.wait()

    ids = lax.broadcasted_iota(jnp.int32, (rim, side), 0)

    def cut_far(s, rank):
        step = steps[s]
        row, col = corner(around[s], step.peer_upper, rank)
        top = row + step.peer_offset + step.peer_far_low + rim
        return [cut_window(ext, plane, top, col, rim, side) for plane in range(2)]

    def mixed(s, rank, j, plane):
        step = steps[s]
        row, col = corner(here, step.upper, rank)
        held = cut_window(ext, plane, row + rim + step.far_low, col, rim, side)
        rows = ids + (row + step.far_low)
        outside = jnp.logical_or(rows < 0, rows >= band_rows)
        return jnp.where(outside, far_in[s, j, plane].astype(jnp.float32), held)

    def near_half(s, rank, plane):
        step = steps[s]
        row, col = corner(here, step.upper, rank)
        return cut_window(ext, plane, row + rim + step.near_low, col, rim, side)

    def send_near(s):
        for plane in range(2):
            x_send[s, plane, near[s]] = near_half(s, other_cut, plane).astype(jnp.bfloat16)
        x_near[s].start()

    def send_halo(s):
        for note in notes[s]:
            note.wait()
        for j, rank in enumerate((other_cut, c)):
            for plane, part in enumerate(cut_far(s, rank)):
                far_send[s, j, plane] = part.astype(jnp.bfloat16)
            halo[s][j].start()

    def send_far(s):
        halo[s][0].wait_recv()
        for plane in range(2):
            x_send[s, plane, far[s]] = mixed(s, other_cut, 0, plane).astype(jnp.bfloat16)
        x_far[s].start()

    def gather_own(s):
        halo[s][1].wait_recv()
        for plane in range(2):
            own[s, plane, near[s]] = near_half(s, c, plane)
            own[s, plane, far[s]] = mixed(s, c, 1, plane)

    send_near(0)
    send_halo(0)
    send_far(0)
    send_near(1)
    send_halo(1)
    for load in loads[3:]:
        load.wait()
    wave[0] = jnp.cos(phase[...])
    wave[1] = jnp.sin(phase[...])
    for k, (s, rank) in enumerate(((0, c), (0, other_cut), (1, c), (1, other_cut))):
        row, col = corner(here, steps[s].upper, rank)
        coords[2 * k] = row
        coords[2 * k + 1] = col
    for k, (s, rank) in enumerate(((0, c), (0, other_cut), (1, c), (1, other_cut))):
        row, col = corner(around[s], steps[s].peer_upper, rank)
        coords[8 + 2 * k] = row + steps[s].peer_offset + steps[s].peer_far_low
        coords[9 + 2 * k] = col
    gather_own(0)
    first = c == 0

    @pl.when(jnp.logical_not(steps[1].wraps))
    def _():
        send_far(1)

    for s in range(2):
        step = steps[s]
        position = find(here[0], step.upper, c)
        psi0 = wide(probes, choice[position])
        x_near[s].wait_recv()
        x_far[s].wait_recv()
        mine = tuple(own[s, plane] for plane in range(2))
        theirs = tuple(x_in[s, plane].astype(jnp.float32) for plane in range(2))
        object0 = tuple(jnp.where(first, x, y) for x, y in zip(mine, theirs))
        object1 = tuple(jnp.where(first, y, x) for x, y in zip(mine, theirs))
        d0, d1 = one_position(psi0, object0, object1, amps[position], (wave[0], wave[1]), tables)
        for plane in range(2):
            give[s, plane] = jnp.where(first, d1[plane], d0[plane]).astype(jnp.bfloat16)
        give_far[s].start()
        give_near[s].start()
        for plane in range(2):
            keep[s, plane] = jnp.where(first, d0[plane], d1[plane]).astype(jnp.bfloat16)
        back_own[s].start()
        if s == 0:

            @pl.when(steps[1].wraps)
            def _():
                send_far(1)

            gather_own(1)
    for s in range(2):
        give_far[s].wait_recv()
        back_other[s].start()
    for copy in x_near + x_far + halo[0] + halo[1] + give_far:
        copy.wait_send()
    for copy in give_near + back_own + back_other:
        copy.wait()


def deposit_kernel(side, coords, keep, give_in, far_back, out, grad, out_sem):
    rim = side // 2
    quarter = side // 4
    band_rows = out.shape[1]
    region = lax.axis_index("region")
    grad[...] = jnp.zeros_like(grad)
    stores = []
    for plane in range(2):
        for s in range(2):
            even = 1 - lax.rem(region, 2)
            upper = 1 - even if s == 0 else even
            low = pl.multiple_of(upper * quarter, quarter)
            rows = pl.ds(low, side - quarter)
            parts = [
                (keep[s, plane, rows], coords[4 * s] + low, coords[4 * s + 1]),
                (give_in[s, plane, rows], coords[4 * s + 2] + low, coords[4 * s + 3]),
                (far_back[s, 0, plane], coords[8 + 4 * s], coords[9 + 4 * s]),
                (far_back[s, 1, plane], coords[10 + 4 * s], coords[11 + 4 * s]),
            ]
            for part, row, col in parts:
                add_window(grad, plane, row + rim, col, part.astype(jnp.float32))
        stores.append(
            pltpu.make_async_copy(
                grad.at[plane, pl.ds(rim, band_rows)], out.at[plane], out_sem.at[plane]
            )
        )
        stores[-1].start()
    for store in stores:
        store.wait()


def shards(objects, probes, amplitudes, prop_phase, scan_rows, scan_cols, probe_choice):
    side = probes.shape[-1]
    rim = side // 2
    count = lax.axis_size("region")
    band = objects[0]
    band_rows, columns = band.shape[1:]
    tables = dft_blocks(side)
    whole = (2, 2, side, side)
    half = (2, 2, 2, rim, side)
    held = lambda shape: jax.ShapeDtypeStruct(shape, jnp.bfloat16)
    slot = lambda shape: pltpu.VMEM(shape, jnp.bfloat16)
    tall = pltpu.VMEM((2, band_rows + 2 * rim + SUBLANES, columns), jnp.float32)
    ANY = pl.BlockSpec(memory_space=pl.ANY)
    scalars = pltpu.SMEM(scan_rows.shape, jnp.int32)
    coords, keep, give_in, far_back = pl.pallas_call(
        functools.partial(wave_kernel, side, count),
        out_shape=(jax.ShapeDtypeStruct((16,), jnp.int32), held(whole), held(whole), held(half)),
        in_specs=[(ANY, ANY)] + [ANY] * 6,
        out_specs=(SMEM, VMEM, VMEM, VMEM),
        scratch_shapes=[
            tall,
            pltpu.VMEM(probes.shape, probes.dtype),
            pltpu.VMEM(amplitudes.shape, amplitudes.dtype),
            pltpu.VMEM(prop_phase.shape, jnp.float32),
            pltpu.VMEM((2,) + prop_phase.shape, jnp.float32),
            pltpu.VMEM(tables.shape, tables.dtype),
            slot(whole), slot(whole), slot(half), slot(half),
            pltpu.VMEM(whole, jnp.float32), slot(whole),
            (scalars,) * 2, ((scalars,) * 2,) * 2, scalars,
            pltpu.SemaphoreType.DMA((8,)),
            pltpu.SemaphoreType.DMA((24,)),
            pltpu.SemaphoreType.DMA((24,)),
        ],
        compiler_params=pltpu.CompilerParams(
            collective_id=0, has_side_effects=True, vmem_limit_bytes=60000 * 1024
        ),
    )((scan_rows, scan_cols), probe_choice, band, probes, amplitudes, prop_phase, tables)
    out = pl.pallas_call(
        functools.partial(deposit_kernel, side),
        out_shape=jax.ShapeDtypeStruct(band.shape, jnp.float32),
        in_specs=[SMEM] + [VMEM] * 3,
        out_specs=ANY,
        scratch_shapes=[tall, pltpu.SemaphoreType.DMA((2,))],
        compiler_params=LIMIT,
    )(coords, keep, give_in, far_back)
    return out[None]


def solution(mesh):
    return jax.shard_map(
        shards,
        mesh=mesh,
        in_specs=(
            P("cuts", None, "region", None),
            P(),
            P("region", None, None),
            P(),
            P("region"),
            P("region"),
            P("region"),
        ),
        out_specs=P("cuts", None, "region", None),
        check_vma=False,
    )
```

time: 41.3 us -> 45.4 us (1.099)
  the two profiles are of different devices: /device:TPU:1 before, /device:TPU:0 now
where the time goes in v1:
time: 45.4 us; the launch traced here: 45.2 us
  Pallas kernels  45.2 us (100%)
    pallas_call x1, Pallas kernels, shards(): pl.pallas_call(functools.partial(wave_kernel, side, count), out_shape=(ja...  41.3 us
    pallas_call x1, Pallas kernels, shards(): pl.pallas_call(functools.partial(deposit_kernel, side), out_shape=jax.Sha...  3.92 us

profile of v1, /device:TPU:0, one launch (start us, length us, event | category | flops | bytes accessed | tf_op | source)
XLA Modules:
  0.0 45.2 jit_solution(2281770424843926442)
XLA Ops:
  0.0 41.3 %shard_map.82 = (s32[16]{0:T(128)}, bf16[2,2,256,256]{3,2,1,0:T(8,128)(2,1)}, bf16[2,2,256,256]{3,2,1,0:T(8,128)(2,1)}, bf16[2,2,2,128,256]{4,3,2,1,0:T(8,128)(2,1)}) custom-call(s32[4]{0:T(128)} %scans_0_.1, s32[4]{0:T(128)} %scans_1_.1, s32[4]{0:T(128)} %choice_any.1, f32[2,256,1024]{2,1,0:T(8,128)} %bitcast.2, bf16[4,2,256,256]{3,2,1,0:T(8,128)(2,1)} %probes_any.1, ...), custom_call_target="tpu_custom_call" | custom-call | tf_op jit(solution)/shard_map/pallas_call | solution.py:360
  41.3 3.9 %shard_map.83 = f32[2,256,1024]{2,1,0:T(8,128)} custom-call(s32[16]{0:T(128)} %get-tuple-element.9.coords, bf16[2,2,256,256]{3,2,1,0:T(8,128)(2,1)} %get-tuple-element.10.keep, bf16[2,2,256,256]{3,2,1,0:T(8,128)(2,1)} %get-tuple-element.11.give_in, bf16[2,2,2,128,256]{4,3,2,1,0:T(8,128)(2,1)} %get-tuple-element.12.far_back), custom_call_target="tpu_custom_call" | custom-call | tf_op jit(solution)/shard_map/pallas_call | solution.py:383

commit v2 on v1

--- a/solution.py
+++ b/solution.py
@@ -1,3 +1,4 @@
+import contextlib
 import functools
 import jax
 import jax.numpy as jnp
@@ -12,15 +13,26 @@
 SUBLANES = 8
 VMEM = pl.BlockSpec(memory_space=pltpu.VMEM)
 SMEM = pl.BlockSpec(memory_space=pltpu.SMEM)
-LIMIT = pltpu.CompilerParams(vmem_limit_bytes=60000 * 1024)
+LIMIT = pltpu.CompilerParams(vmem_limit_bytes=16 * 1024 * 1024)
+
+
+def mark(name):
+    return contextlib.nullcontext()
 
 
 def dft_blocks(side):
+    half = side // 2
     indices = np.arange(side)
     angles = (indices[:, None] * indices[None, :] % side) * (2.0 * np.pi / side)
     real = np.cos(angles) / np.sqrt(side)
     imag = np.sin(angles) / np.sqrt(side)
-    tables = [np.block([[real, imag], [-imag, real]]), np.block([[real, -imag], [imag, real]])]
+    tables = []
+    for odd in range(2):
+        cos, sin = real[:half, odd::2], imag[:half, odd::2]
+        tables.append(np.block([[cos.T, sin.T], [-sin.T, cos.T]]))
+    for odd in range(2):
+        cos, sin = real[:half, odd::2], imag[:half, odd::2]
+        tables.append(np.block([[cos, -sin], [sin, cos]]))
     return jnp.asarray(np.stack(tables), dtype=jnp.bfloat16)
 
 
@@ -70,13 +82,75 @@
     return jnp.dot(left, right, preferred_element_type=jnp.float32)
 
 
-def transform(field, tables, which):
-    side = field[0].shape[0]
-    stacked = jnp.concatenate([field[0].astype(jnp.bfloat16), field[1].astype(jnp.bfloat16)], axis=0)
-    middle = dot(tables[which], stacked).astype(jnp.bfloat16)
-    beside = jnp.concatenate([middle[:side], middle[side:]], axis=1)
-    result = dot(beside, tables[1 - which])
-    return result[:, :side], result[:, side:]
+def narrow(left, right, axis):
+    return jnp.concatenate([left, right], axis=axis).astype(jnp.bfloat16)
+
+
+def forward(field, tables):
+    half = field[0].shape[0] // 2
+    low, high = [part[:half] for part in field], [part[half:] for part in field]
+    even = dot(tables[0], narrow(low[0] + high[0], low[1] + high[1], 0))
+    odd = dot(tables[1], narrow(low[0] - high[0], low[1] - high[1], 0))
+    middle = [
+        jnp.concatenate([even[:half], odd[:half]], axis=0),
+        jnp.concatenate([even[half:], odd[half:]], axis=0),
+    ]
+    low, high = [part[:, :half] for part in middle], [part[:, half:] for part in middle]
+    even = dot(narrow(low[0] + high[0], low[1] + high[1], 1), tables[2])
+    odd = dot(narrow(low[0] - high[0], low[1] - high[1], 1), tables[3])
+    return (
+        jnp.concatenate([even[:, :half], odd[:, :half]], axis=1),
+        jnp.concatenate([even[:, half:], odd[:, half:]], axis=1),
+    )
+
+
+def inverse(field, tables):
+    half = field[0].shape[0] // 2
+    even = dot(tables[2], narrow(field[0][:half], field[1][:half], 0))
+    odd = dot(tables[3], narrow(field[0][half:], field[1][half:], 0))
+    total, rest = even + odd, even - odd
+    middle = [
+        jnp.concatenate([total[:half], rest[:half]], axis=0),
+        jnp.concatenate([total[half:], rest[half:]], axis=0),
+    ]
+    even = dot(narrow(middle[0][:, :half], middle[1][:, :half], 1), tables[0])
+    odd = dot(narrow(middle[0][:, half:], middle[1][:, half:], 1), tables[1])
+    total, rest = even + odd, even - odd
+    return (
+        jnp.concatenate([total[:, :half], rest[:, :half]], axis=1),
+        jnp.concatenate([total[:, half:], rest[:, half:]], axis=1),
+    )
+
+
+def even_first(rows):
+    array = jnp.concatenate(
+        [jnp.concatenate([rows(first, k) for k in range(2)], axis=1) for first in range(2)], axis=0
+    )
+    side = array.shape[1]
+    source = lax.broadcasted_iota(jnp.int32, (side, side), 0)
+    target = lax.broadcasted_iota(jnp.int32, (side, side), 1)
+    wanted = jnp.where(target < side // 2, 2 * target, 2 * target - side + 1)
+    pick = jnp.where(source == wanted, 1.0, 0.0).astype(jnp.bfloat16)
+    total = None
+    for _ in range(3):
+        part = array.astype(jnp.bfloat16)
+        array = array - part.astype(jnp.float32)
+        moved = dot(part, pick)
+        total = moved if total is None else total + moved
+    return total
+
+
+def turn(phase):
+    x = phase * 0.5
+    y = x * x
+    sin = np.float32(1.0 / 6227020800.0)
+    for factor in (-39916800.0, 362880.0, -5040.0, 120.0, -6.0, 1.0):
+        sin = sin * y + np.float32(1.0 / factor)
+    sin = sin * x
+    cos = np.float32(-1.0 / 87178291200.0)
+    for factor in (479001600.0, -3628800.0, 40320.0, -720.0, 24.0, -2.0, 1.0):
+        cos = cos * y + np.float32(1.0 / factor)
+    return 1.0 - 2.0 * sin * sin, 2.0 * sin * cos
 
 
 def multiply(left, right):
@@ -93,15 +167,15 @@
 
 def one_position(psi0, object0, object1, measured, wave, tables):
     psi1 = narrowed(
-        transform(multiply(wave, transform(multiply(psi0, object0), tables, 0)), tables, 1)
-    )
-    far = transform(multiply(psi1, object1), tables, 0)
+        inverse(multiply(wave, forward(multiply(psi0, object0), tables)), tables)
+    )
+    far = forward(multiply(psi1, object1), tables)
     modulus = jnp.sqrt(far[0] * far[0] + far[1] * far[1])
     factor = 1.0 - measured / jnp.maximum(modulus, modulus_floor)
-    g1 = narrowed(transform((far[0] * factor, far[1] * factor), tables, 1))
+    g1 = narrowed(inverse((far[0] * factor, far[1] * factor), tables))
     d1 = multiply_conjugate(psi1, g1)
-    back = transform(multiply_conjugate(object1, g1), tables, 0)
-    g0 = narrowed(transform(multiply_conjugate(wave, back), tables, 1))
+    back = forward(multiply_conjugate(object1, g1), tables)
+    g0 = narrowed(inverse(multiply_conjugate(wave, back), tables))
     return multiply_conjugate(psi0, g0), d1
 
 
@@ -145,11 +219,11 @@
 
 def wave_kernel(
     side, count, scans, choice_any, band, probes_any, amps_any, phase_any, tables_any,
-    coords, keep, give_in, far_back,
-    ext, probes, amps, phase, wave, tables,
-    x_send, x_in, far_send, far_in, own, give,
+    coords, keep_out, give_in, far_back,
+    ext, probes, amps, phase, wave, tables, measured,
+    x_send, x_in, far_send, far_in, own, give, keep,
     here, around, choice,
-    local_sem, send_sem, recv_sem,
+    local_sem, keep_sem, send_sem, recv_sem,
 ):
     rim = side // 2
     band_rows = band.shape[1]
@@ -161,8 +235,10 @@
         pltpu.make_async_copy(source, target, local_sem.at[k])
         for k, (source, target) in enumerate((
             (scans[0], here[0]), (scans[1], here[1]),
-            (band, ext.at[:, pl.ds(rim, band_rows)]), (choice_any, choice), (phase_any, phase),
-            (tables_any, tables), (probes_any, probes), (amps_any, amps),
+            (band, ext.at[:, pl.ds(rim, band_rows)]), (choice_any, choice),
+            (tables_any, tables), (probes_any, probes),
+            *((phase_any.at[:, pl.ds(k * rim, rim)], phase.at[k]) for k in range(2)),
+            *((amps_any.at[:, :, pl.ds(k * rim, rim)], amps.at[k]) for k in range(2)),
         ))
     ]
     for load in loads:
@@ -171,7 +247,8 @@
     peers = [(other_cut, region)] + [(c, step.peer) for step in steps]
     for peer in peers:
         pl.semaphore_signal(barrier, 1, device_id=peer, device_id_type=pl.DeviceIdType.MESH)
-    pl.semaphore_wait(barrier, len(peers))
+    with mark("bar"):
+        pl.semaphore_wait(barrier, len(peers))
     slots = iter(range(24))
 
     def remote(source, target, peer):
@@ -195,7 +272,13 @@
         for s in range(2)
     ]
     give_far = [remote(give.at[s, :, far[s]], give_in.at[s, :, far[s]], across) for s in range(2)]
-    give_near = [remote(give.at[s, :, near[s]], give_in.at[s, :, near[s]], across) for s in range(2)]
+    give_near = []
+    for s in range(2):
+        rows = [pl.ds(pl.multiple_of(steps[s].near_low + k * rim // 2, rim // 2), rim // 2) for k in range(2)]
+        give_near.append(
+            [remote(give.at[s, :, part], give_in.at[s, :, part], across) for part in rows]
+        )
+    keeps = [pltpu.make_async_copy(keep.at[s], keep_out.at[s], keep_sem.at[s]) for s in range(2)]
     back_own = [
         remote(keep.at[s, :, far[s]], far_back.at[s, 0], (c, steps[s].peer)) for s in range(2)
     ]
@@ -205,8 +288,9 @@
     for pair in notes:
         for note in pair:
             note.start()
-    for load in loads[:3]:
-        load.wait()
+    with mark("band"):
+        for load in loads[:3]:
+            load.wait()
 
     ids = lax.broadcasted_iota(jnp.int32, (rim, side), 0)
 
@@ -229,40 +313,57 @@
         row, col = corner(here, step.upper, rank)
         return cut_window(ext, plane, row + rim + step.near_low, col, rim, side)
 
-    def send_near(s):
+    def cut_near(s):
         for plane in range(2):
             x_send[s, plane, near[s]] = near_half(s, other_cut, plane).astype(jnp.bfloat16)
-        x_near[s].start()
-
-    def send_halo(s):
-        for note in notes[s]:
-            note.wait()
-        for j, rank in enumerate((other_cut, c)):
-            for plane, part in enumerate(cut_far(s, rank)):
-                far_send[s, j, plane] = part.astype(jnp.bfloat16)
-            halo[s][j].start()
+
+    def cut_halo(s, j):
+        for plane, part in enumerate(cut_far(s, (other_cut, c)[j])):
+            far_send[s, j, plane] = part.astype(jnp.bfloat16)
 
     def send_far(s):
-        halo[s][0].wait_recv()
+        with mark("wh0"):
+            halo[s][0].wait_recv()
         for plane in range(2):
             x_send[s, plane, far[s]] = mixed(s, other_cut, 0, plane).astype(jnp.bfloat16)
         x_far[s].start()
 
     def gather_own(s):
-        halo[s][1].wait_recv()
+        with mark("wh1"):
+            halo[s][1].wait_recv()
         for plane in range(2):
             own[s, plane, near[s]] = near_half(s, c, plane)
             own[s, plane, far[s]] = mixed(s, c, 1, plane)
 
-    send_near(0)
-    send_halo(0)
-    send_far(0)
-    send_near(1)
-    send_halo(1)
-    for load in loads[3:]:
-        load.wait()
-    wave[0] = jnp.cos(phase[...])
-    wave[1] = jnp.sin(phase[...])
+    with mark("near0"):
+        cut_near(0)
+        x_near[0].start()
+    for s in range(2):
+        with mark("wnote"):
+            for note in notes[s]:
+                note.wait()
+        if s == 0:
+            for j in range(2):
+                cut_halo(0, j)
+                halo[0][j].start()
+            with mark("far0"):
+                send_far(0)
+        else:
+            cut_halo(1, 0)
+            halo[1][0].start()
+    with mark("prep"):
+        cut_near(1)
+        for load in loads[3:]:
+            load.wait()
+        wave[0], wave[1] = turn(
+            even_first(lambda first, k: phase[k, pl.ds(first, rim, stride=2), :])
+        )
+        gather_own(0)
+        for s in range(2):
+            position = find(here[0], steps[s].upper, c)
+            measured[s] = even_first(
+                lambda first, k: amps[k, position, pl.ds(first, rim, stride=2), :]
+            )
     for k, (s, rank) in enumerate(((0, c), (0, other_cut), (1, c), (1, other_cut))):
         row, col = corner(here, steps[s].upper, rank)
         coords[2 * k] = row
@@ -271,44 +372,71 @@
         row, col = corner(around[s], steps[s].peer_upper, rank)
         coords[8 + 2 * k] = row + steps[s].peer_offset + steps[s].peer_far_low
         coords[9 + 2 * k] = col
-    gather_own(0)
     first = c == 0
+    with mark("wsA"):
+        x_near[0].wait_send()
+        x_far[0].wait_send()
+    x_near[1].start()
+    cut_halo(1, 1)
+    halo[1][1].start()
 
     @pl.when(jnp.logical_not(steps[1].wraps))
     def _():
-        send_far(1)
+        with mark("far1"):
+            send_far(1)
 
     for s in range(2):
         step = steps[s]
         position = find(here[0], step.upper, c)
         psi0 = wide(probes, choice[position])
-        x_near[s].wait_recv()
-        x_far[s].wait_recv()
+        with mark("wx"):
+            x_near[s].wait_recv()
+            x_far[s].wait_recv()
         mine = tuple(own[s, plane] for plane in range(2))
         theirs = tuple(x_in[s, plane].astype(jnp.float32) for plane in range(2))
         object0 = tuple(jnp.where(first, x, y) for x, y in zip(mine, theirs))
         object1 = tuple(jnp.where(first, y, x) for x, y in zip(mine, theirs))
-        d0, d1 = one_position(psi0, object0, object1, amps[position], (wave[0], wave[1]), tables)
+        with mark("pos"):
+            d0, d1 = one_position(psi0, object0, object1, measured[s], (wave[0], wave[1]), tables)
         for plane in range(2):
             give[s, plane] = jnp.where(first, d1[plane], d0[plane]).astype(jnp.bfloat16)
-        give_far[s].start()
-        give_near[s].start()
-        for plane in range(2):
             keep[s, plane] = jnp.where(first, d0[plane], d1[plane]).astype(jnp.bfloat16)
-        back_own[s].start()
         if s == 0:
+            back_own[0].start()
+            keeps[0].start()
 
             @pl.when(steps[1].wraps)
             def _():
-                send_far(1)
-
-            gather_own(1)
+                with mark("far1w"):
+                    send_far(1)
+
+            with mark("own1"):
+                gather_own(1)
+            with mark("wsB"):
+                x_near[1].wait_send()
+                x_far[1].wait_send()
+            give_far[0].start()
+            give_near[0][0].start()
+        else:
+            give_far[1].start()
+            give_near[0][1].start()
+            give_near[1][0].start()
+            give_near[1][1].start()
+            back_own[1].start()
+            keeps[1].start()
     for s in range(2):
-        give_far[s].wait_recv()
+        with mark("wgf"):
+            give_far[s].wait_recv()
         back_other[s].start()
-    for copy in x_near + x_far + halo[0] + halo[1] + give_far:
+    for copy in halo[0] + halo[1] + give_far:
         copy.wait_send()
-    for copy in give_near + back_own + back_other:
+    with mark("wgn"):
+        for copy in give_near[0] + give_near[1]:
+            copy.wait()
+    with mark("wend"):
+        for copy in back_own + back_other:
+            copy.wait()
+    for copy in keeps:
         copy.wait()
 
 
@@ -356,30 +484,33 @@
     slot = lambda shape: pltpu.VMEM(shape, jnp.bfloat16)
     tall = pltpu.VMEM((2, band_rows + 2 * rim + SUBLANES, columns), jnp.float32)
     ANY = pl.BlockSpec(memory_space=pl.ANY)
+    HBM = pl.BlockSpec(memory_space=pltpu.HBM)
     scalars = pltpu.SMEM(scan_rows.shape, jnp.int32)
     coords, keep, give_in, far_back = pl.pallas_call(
         functools.partial(wave_kernel, side, count),
         out_shape=(jax.ShapeDtypeStruct((16,), jnp.int32), held(whole), held(whole), held(half)),
-        in_specs=[(ANY, ANY)] + [ANY] * 6,
-        out_specs=(SMEM, VMEM, VMEM, VMEM),
+        in_specs=[(HBM, HBM)] + [HBM] * 6,
+        out_specs=(SMEM, ANY, ANY, ANY),
         scratch_shapes=[
             tall,
             pltpu.VMEM(probes.shape, probes.dtype),
-            pltpu.VMEM(amplitudes.shape, amplitudes.dtype),
-            pltpu.VMEM(prop_phase.shape, jnp.float32),
+            pltpu.VMEM((2,) + amplitudes.shape[:2] + (rim,), jnp.float32),
+            pltpu.VMEM((2, side, rim), jnp.float32),
             pltpu.VMEM((2,) + prop_phase.shape, jnp.float32),
             pltpu.VMEM(tables.shape, tables.dtype),
+            pltpu.VMEM((2, side, side), jnp.float32),
             slot(whole), slot(whole), slot(half), slot(half),
-            pltpu.VMEM(whole, jnp.float32), slot(whole),
+            pltpu.VMEM(whole, jnp.float32), slot(whole), slot(whole),
             (scalars,) * 2, ((scalars,) * 2,) * 2, scalars,
-            pltpu.SemaphoreType.DMA((8,)),
+            pltpu.SemaphoreType.DMA((10,)),
+            pltpu.SemaphoreType.DMA((2,)),
             pltpu.SemaphoreType.DMA((24,)),
             pltpu.SemaphoreType.DMA((24,)),
         ],
         compiler_params=pltpu.CompilerParams(
-            collective_id=0, has_side_effects=True, vmem_limit_bytes=60000 * 1024
+            collective_id=0, has_side_effects=True, vmem_limit_bytes=28 * 1024 * 1024
         ),
-    )((scan_rows, scan_cols), probe_choice, band, probes, amplitudes, prop_phase, tables)
+    )(*jax.tree.map(lambda x: pltpu.with_memory_space_constraint(x, pltpu.HBM), ((scan_rows, scan_cols), probe_choice, band, probes, amplitudes, prop_phase, tables)))
     out = pl.pallas_call(
         functools.partial(deposit_kernel, side),
         out_shape=jax.ShapeDtypeStruct(band.shape, jnp.float32),

time: 45.4 us -> 36.2 us (0.80)
  Pallas kernels: 45.2 us -> 36 us
    pallas_call x1, Pallas kernels: 41.3 us -> 33 us  [shards(): pl.pallas_call(functools.partial(wave_kernel, side, count), out_shape=(ja...]
    pallas_call x1, Pallas kernels: 3.92 us -> 3.09 us  [shards(): pl.pallas_call(functools.partial(deposit_kernel, side), out_shape=jax.Sha...]
where the time goes in v2:
time: 36.2 us; the launch traced here: 36.1 us
  Pallas kernels  36 us (99%)
    pallas_call x1, Pallas kernels, shards(): pl.pallas_call(functools.partial(wave_kernel, side, count), out_shape=(ja...  33 us
    pallas_call x1, Pallas kernels, shards(): pl.pallas_call(functools.partial(deposit_kernel, side), out_shape=jax.Sha...  3.09 us

profile of v2, /device:TPU:0, one launch (start us, length us, event | category | flops | bytes accessed | tf_op | source)
XLA Modules:
  0.0 36.1 jit_solution(15002582365436288995)
XLA Ops:
  0.0 33.0 %shard_map.82 = (s32[16]{0:T(128)S(1)}, bf16[2,2,256,256]{3,2,1,0:T(8,128)(2,1)S(1)}, bf16[2,2,256,256]{3,2,1,0:T(8,128)(2,1)S(1)}, bf16[2,2,2,128,256]{4,3,2,1,0:T(8,128)(2,1)S(1)}) custom-call(s32[4]{0:T(128)} %scans_0_.1, s32[4]{0:T(128)} %scans_1_.1, s32[4]{0:T(128)} %choice_any.1, f32[2,256,1024]{2,1,0:T(8,128)} %bitcast.2, ...), custom_call_target="tpu_custom_call" | custom-call | tf_op jit(solution)/shard_map/pallas_call | solution.py:489
  33.0 3.1 %shard_map.83 = f32[2,256,1024]{2,1,0:T(8,128)} custom-call(s32[16]{0:T(128)S(1)} %get-tuple-element.9.coords, bf16[2,2,256,256]{3,2,1,0:T(8,128)(2,1)S(1)} %get-tuple-element.10.keep, bf16[2,2,256,256]{3,2,1,0:T(8,128)(2,1)S(1)} %get-tuple-element.11.give_in, bf16[2,2,2,128,256]{4,3,2,1,0:T(8,128)(2,1)S(1)} %get-tuple-element.12.far_back), custom_call_target="tpu_custom_call" | custom-call | tf_op jit(solution)/shard_map/pallas_call | solution.py:514

commit v3 on v2

--- a/solution.py
+++ b/solution.py
@@ -12,8 +12,6 @@
 LANES = 128
 SUBLANES = 8
 VMEM = pl.BlockSpec(memory_space=pltpu.VMEM)
-SMEM = pl.BlockSpec(memory_space=pltpu.SMEM)
-LIMIT = pltpu.CompilerParams(vmem_limit_bytes=16 * 1024 * 1024)
 
 
 def mark(name):
@@ -58,24 +56,34 @@
     )
 
 
-def add_window(grad, plane, row, col, field):
+def lay_window(padded, plane, row, col, field):
     height, side = field.shape
-    base, shift = split_col(col, grad.shape[2], side)
-    top = lax.div(row, SUBLANES) * SUBLANES
+    rows = lax.rem(row + 8 * SUBLANES * side, SUBLANES)
+    base, shift = col
     tall = height + SUBLANES
     field = jnp.concatenate([field, jnp.zeros((SUBLANES, side), field.dtype)], axis=0)
-    field = pltpu.roll(field, row - top, axis=0)
+    field = pltpu.roll(field, rows, axis=0)
     ahead = lax.rem(shift, LANES)
     chunks = [pltpu.roll(field[:, j : j + LANES], ahead, axis=1) for j in range(0, side, LANES)]
     lane = lax.broadcasted_iota(jnp.int32, (tall, LANES), 1)
     keep = lane >= shift
     zero = jnp.zeros((tall, LANES), field.dtype)
     parts = [zero] + chunks + [zero]
-    placed = jnp.concatenate(
-        [jnp.where(keep, parts[j + 1], parts[j]) for j in range(len(chunks) + 1)], axis=1
-    )
-    where = (plane, pl.ds(top, tall), pl.ds(base, side + LANES))
-    grad[where] = grad[where] + placed
+    for j in range(len(chunks) + 1):
+        padded[plane, j + 1, pl.ds(side // 4, tall)] = jnp.where(keep, parts[j + 1], parts[j])
+
+
+def add_laid(total, padded, plane, row, col, first, height, side):
+    base, _ = col
+    shift = side // 4 + 8 * SUBLANES * side
+    start = (lax.div(first + shift, SUBLANES) - lax.div(row + 8 * SUBLANES * side, SUBLANES)) * SUBLANES
+    count = side // LANES + 1
+    for j in range(total.shape[2] // LANES):
+        block = j - lax.div(base, LANES)
+        inside = jnp.logical_and(block >= 0, block < count)
+        source = padded[plane, jnp.where(inside, block + 1, 0), pl.ds(start, height)]
+        where = (plane, pl.ds(first, height), pl.ds(j * LANES, LANES))
+        total[where] = total[where] + source
 
 
 def dot(left, right):
@@ -193,9 +201,11 @@
     return chosen
 
 
-def corner(info, upper, rank):
+def corner(info, upper, rank, side, band_rows):
     position = find(info[0], upper, rank)
-    return info[0][position], info[1][position]
+    least = jnp.where(upper == 1, -(side // 2), band_rows - side + side // 4)
+    row = jnp.minimum(jnp.maximum(info[0][position], least), least + side // 4)
+    return row, info[1][position]
 
 
 class Step:
@@ -212,18 +222,15 @@
         self.peer_upper = 1 - self.upper
         self.peer_offset = (2 * self.peer_upper - 1) * band_rows
         self.peer_far_low = self.near_low
-        self.wraps = jnp.logical_and(self.upper == 1, region == 0) | jnp.logical_and(
-            self.upper == 0, region == count - 1
-        )
 
 
 def wave_kernel(
     side, count, scans, choice_any, band, probes_any, amps_any, phase_any, tables_any,
-    coords, keep_out, give_in, far_back,
+    total,
     ext, probes, amps, phase, wave, tables, measured,
-    x_send, x_in, far_send, far_in, own, give, keep,
-    here, around, choice,
-    local_sem, keep_sem, send_sem, recv_sem,
+    x_send, x_in, far_send, far_in, own, give, keep, give_in, far_back, strip_send, strip_in,
+    near_laid, far_laid, end_laid, here, around, choice,
+    local_sem, send_sem, recv_sem,
 ):
     rim = side // 2
     band_rows = band.shape[1]
@@ -244,12 +251,21 @@
     for load in loads:
         load.start()
     barrier = pltpu.get_barrier_semaphore()
-    peers = [(other_cut, region)] + [(c, step.peer) for step in steps]
-    for peer in peers:
+    early = region == 0
+    late = region == count - 1
+    wraps = jnp.logical_or(early, late)
+    for peer in ((other_cut, region), (c, steps[0].peer)):
         pl.semaphore_signal(barrier, 1, device_id=peer, device_id_type=pl.DeviceIdType.MESH)
+
+    @pl.when(jnp.logical_not(late))
+    def _():
+        pl.semaphore_signal(
+            barrier, 1, device_id=(c, steps[1].peer), device_id_type=pl.DeviceIdType.MESH
+        )
+
     with mark("bar"):
-        pl.semaphore_wait(barrier, len(peers))
-    slots = iter(range(24))
+        pl.semaphore_wait(barrier, jnp.where(early, 2, 3))
+    slots = iter(range(40))
 
     def remote(source, target, peer):
         slot = next(slots)
@@ -266,28 +282,44 @@
     near = [pl.ds(step.near_low, rim) for step in steps]
     far = [pl.ds(step.far_low, rim) for step in steps]
     x_near = [remote(x_send.at[s, :, near[s]], x_in.at[s, :, near[s]], across) for s in range(2)]
-    x_far = [remote(x_send.at[s, :, far[s]], x_in.at[s, :, far[s]], across) for s in range(2)]
+    x_far = [
+        [remote(x_send.at[s, p, far[s]], x_in.at[s, p, far[s]], across) for p in range(2)]
+        for s in range(2)
+    ]
     halo = [
         [remote(far_send.at[s, j], far_in.at[s, j], (c, steps[s].peer)) for j in range(2)]
         for s in range(2)
     ]
-    give_far = [remote(give.at[s, :, far[s]], give_in.at[s, :, far[s]], across) for s in range(2)]
-    give_near = []
-    for s in range(2):
-        rows = [pl.ds(pl.multiple_of(steps[s].near_low + k * rim // 2, rim // 2), rim // 2) for k in range(2)]
-        give_near.append(
+    quarter = side // 4
+    give_parts, back_other = [], []
+    for s, step in enumerate(steps):
+        order = [3 - k + step.upper * (2 * k - 3) for k in range(4)]
+        rows = [pl.ds(pl.multiple_of(k * quarter, quarter), quarter) for k in order]
+        give_parts.append(
             [remote(give.at[s, :, part], give_in.at[s, :, part], across) for part in rows]
         )
-    keeps = [pltpu.make_async_copy(keep.at[s], keep_out.at[s], keep_sem.at[s]) for s in range(2)]
+        back_other.append([])
+        for part, k in zip(rows[:2], order[:2]):
+            start = pl.multiple_of(k * quarter - step.far_low, quarter)
+            back_other[s].append(
+                remote(
+                    give_in.at[s, :, part],
+                    far_back.at[s, 1, :, pl.ds(start, quarter)],
+                    (c, step.peer),
+                )
+            )
     back_own = [
         remote(keep.at[s, :, far[s]], far_back.at[s, 0], (c, steps[s].peer)) for s in range(2)
     ]
-    back_other = [
-        remote(give_in.at[s, :, far[s]], far_back.at[s, 1], (c, steps[s].peer)) for s in range(2)
-    ]
-    for pair in notes:
-        for note in pair:
+    strip = [remote(strip_send.at[p], strip_in.at[p], (c, steps[1].peer)) for p in range(2)]
+    for note in notes[0]:
+        note.start()
+
+    @pl.when(jnp.logical_not(early))
+    def _():
+        for note in notes[1]:
             note.start()
+
     with mark("band"):
         for load in loads[:3]:
             load.wait()
@@ -296,21 +328,23 @@
 
     def cut_far(s, rank):
         step = steps[s]
-        row, col = corner(around[s], step.peer_upper, rank)
+        row, col = corner(around[s], step.peer_upper, rank, side, band_rows)
         top = row + step.peer_offset + step.peer_far_low + rim
         return [cut_window(ext, plane, top, col, rim, side) for plane in range(2)]
 
     def mixed(s, rank, j, plane):
         step = steps[s]
-        row, col = corner(here, step.upper, rank)
+        row, col = corner(here, step.upper, rank, side, band_rows)
         held = cut_window(ext, plane, row + rim + step.far_low, col, rim, side)
         rows = ids + (row + step.far_low)
         outside = jnp.logical_or(rows < 0, rows >= band_rows)
+        if s == 1:
+            outside = jnp.logical_and(outside, jnp.logical_not(wraps))
         return jnp.where(outside, far_in[s, j, plane].astype(jnp.float32), held)
 
     def near_half(s, rank, plane):
         step = steps[s]
-        row, col = corner(here, step.upper, rank)
+        row, col = corner(here, step.upper, rank, side, band_rows)
         return cut_window(ext, plane, row + rim + step.near_low, col, rim, side)
 
     def cut_near(s):
@@ -321,36 +355,115 @@
         for plane, part in enumerate(cut_far(s, (other_cut, c)[j])):
             far_send[s, j, plane] = part.astype(jnp.bfloat16)
 
-    def send_far(s):
-        with mark("wh0"):
-            halo[s][0].wait_recv()
-        for plane in range(2):
+    def send_far(s, plane):
+        with mark("far"):
             x_send[s, plane, far[s]] = mixed(s, other_cut, 0, plane).astype(jnp.bfloat16)
-        x_far[s].start()
+            x_far[s][plane].start()
+
+    def send_strip_far(plane):
+        with mark("wstrip"):
+            strip[plane].wait_recv()
+        rows = pl.ds(pl.multiple_of((1 - steps[1].upper) * (rim + band_rows), rim), rim)
+        ext[plane, rows] = strip_in[plane].astype(jnp.float32)
+        send_far(1, plane)
 
     def gather_own(s):
-        with mark("wh1"):
-            halo[s][1].wait_recv()
         for plane in range(2):
             own[s, plane, near[s]] = near_half(s, c, plane)
             own[s, plane, far[s]] = mixed(s, c, 1, plane)
 
+    def send_strip():
+        rows = pl.ds(pl.multiple_of(rim + steps[1].peer_upper * (band_rows - rim), rim), rim)
+        for plane in range(2):
+            strip_send[plane] = ext[plane, rows].astype(jnp.bfloat16)
+            strip[plane].start()
+
+    def add_near(s, rank, source):
+        step = steps[s]
+        row, col = corner(here, step.upper, rank, side, band_rows)
+        low = pl.multiple_of(step.upper * quarter, quarter)
+        first = pl.multiple_of((1 - step.upper) * quarter, quarter)
+        place = split_col(col, total.shape[2], side)
+        for plane in range(2):
+            part = source[s, plane, pl.ds(low, side - quarter)].astype(jnp.float32)
+            lay_window(near_laid, plane, row + low, place, part)
+            add_laid(total, near_laid, plane, row + low, place, first, side - quarter, side)
+
+    def add_far(s, j):
+        step = steps[s]
+        row, col = corner(around[s], step.peer_upper, (c, other_cut)[j], side, band_rows)
+        top = row + step.peer_offset + step.peer_far_low
+        first = pl.multiple_of(step.peer_upper * rim, rim)
+        place = split_col(col, total.shape[2], side)
+        for plane in range(2):
+            part = far_back[s, j, plane].astype(jnp.float32)
+            lay_window(far_laid, plane, top, place, part)
+            add_laid(total, far_laid, plane, top, place, first, rim, side)
+
+    def add_middle(s, rank, source):
+        step = steps[s]
+        row, col = corner(here, step.upper, rank, side, band_rows)
+        first = pl.multiple_of((1 - step.upper) * rim, rim)
+        place = split_col(col, total.shape[2], side)
+        for plane in range(2):
+            part = source[s, plane, pl.ds(quarter, rim)].astype(jnp.float32)
+            lay_window(far_laid, plane, row + quarter, place, part)
+            add_laid(total, far_laid, plane, row + quarter, place, first, rim, side)
+
+    def add_end(s, rank, source):
+        step = steps[s]
+        row, col = corner(here, step.upper, rank, side, band_rows)
+        low = pl.multiple_of(step.upper * 3 * quarter, quarter)
+        place = split_col(col, total.shape[2], side)
+        for plane in range(2):
+            part = source[s, plane, pl.ds(low, quarter)].astype(jnp.float32)
+            lay_window(end_laid, plane, row + low, place, part)
+            add_laid(total, end_laid, plane, row + low, place, quarter, rim, side)
+
+    def position_of(s):
+        position = find(here[0], steps[s].upper, c)
+        psi0 = wide(probes, choice[position])
+        with mark("wx"):
+            for copy in [x_near[s]] + x_far[s]:
+                copy.wait_recv()
+        mine = tuple(own[s, plane] for plane in range(2))
+        theirs = tuple(x_in[s, plane].astype(jnp.float32) for plane in range(2))
+        object0 = tuple(jnp.where(first, x, y) for x, y in zip(mine, theirs))
+        object1 = tuple(jnp.where(first, y, x) for x, y in zip(mine, theirs))
+        with mark("pos"):
+            d0, d1 = one_position(psi0, object0, object1, measured[s], (wave[0], wave[1]), tables)
+        for plane in range(2):
+            give[s, plane] = jnp.where(first, d1[plane], d0[plane]).astype(jnp.bfloat16)
+            keep[s, plane] = jnp.where(first, d0[plane], d1[plane]).astype(jnp.bfloat16)
+
+    first = c == 0
     with mark("near0"):
         cut_near(0)
         x_near[0].start()
-    for s in range(2):
+
+    @pl.when(late)
+    def _():
+        send_strip()
+
+    with mark("wnote"):
+        for note in notes[0]:
+            note.wait_recv()
+    for j in range(2):
+        cut_halo(0, j)
+        halo[0][j].start()
+    with mark("wh0"):
+        halo[0][0].wait_recv()
+    for plane in range(2):
+        send_far(0, plane)
+
+    @pl.when(jnp.logical_not(wraps))
+    def _():
         with mark("wnote"):
-            for note in notes[s]:
-                note.wait()
-        if s == 0:
-            for j in range(2):
-                cut_halo(0, j)
-                halo[0][j].start()
-            with mark("far0"):
-                send_far(0)
-        else:
-            cut_halo(1, 0)
-            halo[1][0].start()
+            for note in notes[1]:
+                note.wait_recv()
+        cut_halo(1, 0)
+        halo[1][0].start()
+
     with mark("prep"):
         cut_near(1)
         for load in loads[3:]:
@@ -358,117 +471,132 @@
         wave[0], wave[1] = turn(
             even_first(lambda first, k: phase[k, pl.ds(first, rim, stride=2), :])
         )
+        halo[0][1].wait_recv()
         gather_own(0)
         for s in range(2):
             position = find(here[0], steps[s].upper, c)
             measured[s] = even_first(
                 lambda first, k: amps[k, position, pl.ds(first, rim, stride=2), :]
             )
-    for k, (s, rank) in enumerate(((0, c), (0, other_cut), (1, c), (1, other_cut))):
-        row, col = corner(here, steps[s].upper, rank)
-        coords[2 * k] = row
-        coords[2 * k + 1] = col
-    for k, (s, rank) in enumerate(((0, c), (0, other_cut), (1, c), (1, other_cut))):
-        row, col = corner(around[s], steps[s].peer_upper, rank)
-        coords[8 + 2 * k] = row + steps[s].peer_offset + steps[s].peer_far_low
-        coords[9 + 2 * k] = col
-    first = c == 0
+        near_laid[...] = jnp.zeros_like(near_laid)
+        far_laid[...] = jnp.zeros_like(far_laid)
+        end_laid[...] = jnp.zeros_like(end_laid)
+        total[...] = jnp.zeros_like(total)
+
+    @pl.when(early)
+    def _():
+        with mark("wnote"):
+            for note in notes[1]:
+                note.wait_recv()
+        send_strip()
+        for note in notes[1]:
+            note.start()
+
     with mark("wsA"):
-        x_near[0].wait_send()
-        x_far[0].wait_send()
+        for copy in [x_near[0]] + x_far[0]:
+            copy.wait_send()
     x_near[1].start()
-    cut_halo(1, 1)
-    halo[1][1].start()
-
-    @pl.when(jnp.logical_not(steps[1].wraps))
-    def _():
-        with mark("far1"):
-            send_far(1)
-
-    for s in range(2):
-        step = steps[s]
-        position = find(here[0], step.upper, c)
-        psi0 = wide(probes, choice[position])
-        with mark("wx"):
-            x_near[s].wait_recv()
-            x_far[s].wait_recv()
-        mine = tuple(own[s, plane] for plane in range(2))
-        theirs = tuple(x_in[s, plane].astype(jnp.float32) for plane in range(2))
-        object0 = tuple(jnp.where(first, x, y) for x, y in zip(mine, theirs))
-        object1 = tuple(jnp.where(first, y, x) for x, y in zip(mine, theirs))
-        with mark("pos"):
-            d0, d1 = one_position(psi0, object0, object1, measured[s], (wave[0], wave[1]), tables)
-        for plane in range(2):
-            give[s, plane] = jnp.where(first, d1[plane], d0[plane]).astype(jnp.bfloat16)
-            keep[s, plane] = jnp.where(first, d0[plane], d1[plane]).astype(jnp.bfloat16)
-        if s == 0:
-            back_own[0].start()
-            keeps[0].start()
-
-            @pl.when(steps[1].wraps)
-            def _():
-                with mark("far1w"):
-                    send_far(1)
-
-            with mark("own1"):
-                gather_own(1)
-            with mark("wsB"):
-                x_near[1].wait_send()
-                x_far[1].wait_send()
-            give_far[0].start()
-            give_near[0][0].start()
-        else:
-            give_far[1].start()
-            give_near[0][1].start()
-            give_near[1][0].start()
-            give_near[1][1].start()
-            back_own[1].start()
-            keeps[1].start()
-    for s in range(2):
-        with mark("wgf"):
-            give_far[s].wait_recv()
-        back_other[s].start()
-    for copy in halo[0] + halo[1] + give_far:
+
+    @pl.when(jnp.logical_not(wraps))
+    def _():
+        cut_halo(1, 1)
+        halo[1][1].start()
+        with mark("wh1"):
+            halo[1][0].wait_recv()
+        for plane in range(2):
+            send_far(1, plane)
+
+    @pl.when(wraps)
+    def _():
+        send_strip_far(0)
+
+    position_of(0)
+
+    @pl.when(wraps)
+    def _():
+        send_strip_far(1)
+
+    back_own[0].start()
+
+    @pl.when(jnp.logical_not(wraps))
+    def _():
+        with mark("wh1"):
+            halo[1][1].wait_recv()
+
+    with mark("own1"):
+        gather_own(1)
+    with mark("add"):
+        add_near(0, c, keep)
+    with mark("wsB"):
+        for copy in [x_near[1]] + x_far[1]:
+            copy.wait_send()
+    for copy in give_parts[0]:
+        copy.start()
+    position_of(1)
+    for copy in give_parts[1][:2]:
+        copy.start()
+    back_own[1].start()
+    with mark("wgf0"):
+        for part, back in zip(give_parts[0], back_other[0]):
+            part.wait_recv()
+            back.start()
+    with mark("add"):
+        back_own[0].wait_recv()
+        add_far(0, 0)
+        add_near(1, c, keep)
+
+    @pl.when(late)
+    def _():
+        for note in notes[1]:
+            note.wait_recv()
+
+    with mark("wsC"):
+        give_parts[1][0].wait_send()
+    for copy in give_parts[1][2:]:
+        copy.start()
+    with mark("wgf1"):
+        for part, back in zip(give_parts[1], back_other[1]):
+            part.wait_recv()
+            back.start()
+    with mark("add"):
+        for copy in give_parts[0][2:]:
+            copy.wait_recv()
+        add_near(0, other_cut, give_in)
+    with mark("add"):
+        for copy in back_other[0]:
+            copy.wait_recv()
+        add_far(0, 1)
+    with mark("add"):
+        back_own[1].wait_recv()
+        add_far(1, 0)
+    with mark("wgn"):
+        give_parts[1][2].wait_recv()
+    with mark("add"):
+        add_middle(1, other_cut, give_in)
+    with mark("wgn"):
+        give_parts[1][3].wait_recv()
+    with mark("add"):
+        add_end(1, other_cut, give_in)
+    with mark("wend"):
+        for copy in back_other[1]:
+            copy.wait_recv()
+    with mark("add"):
+        add_far(1, 1)
+
+    @pl.when(wraps)
+    def _():
+        for copy in strip:
+            copy.wait_send()
+
+    @pl.when(jnp.logical_not(wraps))
+    def _():
+        for copy in halo[1]:
+            copy.wait_send()
+
+    for copy in notes[0] + notes[1] + halo[0] + give_parts[0] + give_parts[1][1:]:
         copy.wait_send()
-    with mark("wgn"):
-        for copy in give_near[0] + give_near[1]:
-            copy.wait()
-    with mark("wend"):
-        for copy in back_own + back_other:
-            copy.wait()
-    for copy in keeps:
-        copy.wait()
-
-
-def deposit_kernel(side, coords, keep, give_in, far_back, out, grad, out_sem):
-    rim = side // 2
-    quarter = side // 4
-    band_rows = out.shape[1]
-    region = lax.axis_index("region")
-    grad[...] = jnp.zeros_like(grad)
-    stores = []
-    for plane in range(2):
-        for s in range(2):
-            even = 1 - lax.rem(region, 2)
-            upper = 1 - even if s == 0 else even
-            low = pl.multiple_of(upper * quarter, quarter)
-            rows = pl.ds(low, side - quarter)
-            parts = [
-                (keep[s, plane, rows], coords[4 * s] + low, coords[4 * s + 1]),
-                (give_in[s, plane, rows], coords[4 * s + 2] + low, coords[4 * s + 3]),
-                (far_back[s, 0, plane], coords[8 + 4 * s], coords[9 + 4 * s]),
-                (far_back[s, 1, plane], coords[10 + 4 * s], coords[11 + 4 * s]),
-            ]
-            for part, row, col in parts:
-                add_window(grad, plane, row + rim, col, part.astype(jnp.float32))
-        stores.append(
-            pltpu.make_async_copy(
-                grad.at[plane, pl.ds(rim, band_rows)], out.at[plane], out_sem.at[plane]
-            )
-        )
-        stores[-1].start()
-    for store in stores:
-        store.wait()
+    for copy in back_own + back_other[0] + back_other[1]:
+        copy.wait_send()
 
 
 def shards(objects, probes, amplitudes, prop_phase, scan_rows, scan_cols, probe_choice):
@@ -480,17 +608,16 @@
     tables = dft_blocks(side)
     whole = (2, 2, side, side)
     half = (2, 2, 2, rim, side)
-    held = lambda shape: jax.ShapeDtypeStruct(shape, jnp.bfloat16)
     slot = lambda shape: pltpu.VMEM(shape, jnp.bfloat16)
     tall = pltpu.VMEM((2, band_rows + 2 * rim + SUBLANES, columns), jnp.float32)
-    ANY = pl.BlockSpec(memory_space=pl.ANY)
     HBM = pl.BlockSpec(memory_space=pltpu.HBM)
     scalars = pltpu.SMEM(scan_rows.shape, jnp.int32)
-    coords, keep, give_in, far_back = pl.pallas_call(
+    laid = lambda rows: pltpu.VMEM((2, side // LANES + 2, rows, LANES), jnp.float32)
+    out = pl.pallas_call(
         functools.partial(wave_kernel, side, count),
-        out_shape=(jax.ShapeDtypeStruct((16,), jnp.int32), held(whole), held(whole), held(half)),
+        out_shape=jax.ShapeDtypeStruct(band.shape, jnp.float32),
         in_specs=[(HBM, HBM)] + [HBM] * 6,
-        out_specs=(SMEM, ANY, ANY, ANY),
+        out_specs=VMEM,
         scratch_shapes=[
             tall,
             pltpu.VMEM(probes.shape, probes.dtype),
@@ -500,25 +627,21 @@
             pltpu.VMEM(tables.shape, tables.dtype),
             pltpu.VMEM((2, side, side), jnp.float32),
             slot(whole), slot(whole), slot(half), slot(half),
-            pltpu.VMEM(whole, jnp.float32), slot(whole), slot(whole),
+            pltpu.VMEM(whole, jnp.float32), slot(whole), slot(whole), slot(whole), slot(half),
+            slot((2, rim, columns)), slot((2, rim, columns)),
+            laid(side + side // 4), laid(side), laid(side - side // 4),
             (scalars,) * 2, ((scalars,) * 2,) * 2, scalars,
             pltpu.SemaphoreType.DMA((10,)),
-            pltpu.SemaphoreType.DMA((2,)),
-            pltpu.SemaphoreType.DMA((24,)),
-            pltpu.SemaphoreType.DMA((24,)),
+            pltpu.SemaphoreType.DMA((40,)),
+            pltpu.SemaphoreType.DMA((40,)),
         ],
         compiler_params=pltpu.CompilerParams(
-            collective_id=0, has_side_effects=True, vmem_limit_bytes=28 * 1024 * 1024
+            collective_id=0, has_side_effects=True, vmem_limit_bytes=32 * 1024 * 1024
         ),
-    )(*jax.tree.map(lambda x: pltpu.with_memory_space_constraint(x, pltpu.HBM), ((scan_rows, scan_cols), probe_choice, band, probes, amplitudes, prop_phase, tables)))
-    out = pl.pallas_call(
-        functools.partial(deposit_kernel, side),
-        out_shape=jax.ShapeDtypeStruct(band.shape, jnp.float32),
-        in_specs=[SMEM] + [VMEM] * 3,
-        out_specs=ANY,
-        scratch_shapes=[tall, pltpu.SemaphoreType.DMA((2,))],
-        compiler_params=LIMIT,
-    )(coords, keep, give_in, far_back)
+    )(*jax.tree.map(
+        lambda x: pltpu.with_memory_space_constraint(x, pltpu.HBM),
+        ((scan_rows, scan_cols), probe_choice, band, probes, amplitudes, prop_phase, tables),
+    ))
     return out[None]
 
 

time: 36.2 us -> 35.2 us (0.972)
  Pallas kernels: 36 us -> 33.8 us
  local copies, waits for them, and re-layouts: 0 us -> 1.32 us
    pallas_call x2 -> x1, Pallas kernels: 36 us -> 33.8 us  [shards(): pl.pallas_call(functools.partial(wave_kernel, side, count), out_shape=jax...]
    unnamed x0 -> x1, local copies, waits for them, and re-layouts: none -> 1.32 us
where the time goes in v3:
time: 35.2 us; the launch traced here: 35.1 us
  Pallas kernels  33.8 us (96%)
  local copies, waits for them, and re-layouts  1.32 us (4%)
    pallas_call x1, Pallas kernels, shards(): pl.pallas_call(functools.partial(wave_kernel, side, count), out_shape=jax...  33.8 us
    unnamed x1, local copies, waits for them, and re-layouts  1.32 us

profile of v3, /device:TPU:0, one launch (start us, length us, event | category | flops | bytes accessed | tf_op | source)
XLA Modules:
  0.0 35.1 jit_solution(13476999471679050852)
XLA Ops:
  0.0 33.8 %shard_map.82 = f32[2,256,1024]{2,1,0:T(8,128)S(1)} custom-call(s32[4]{0:T(128)} %scans_0_.1, s32[4]{0:T(128)} %scans_1_.1, s32[4]{0:T(128)} %choice_any.1, f32[2,256,1024]{2,1,0:T(8,128)} %bitcast.3, bf16[4,2,256,256]{3,2,1,0:T(8,128)(2,1)} %probes_any.1, f32[4,256,256]{2,1,0:T(8,128)} %amps_any.1, f32[256,256]{1,0:T(8,128)} %phase_any.1, ...), custom_call_target="tpu_custom_call" | custom-call | tf_op jit(solution)/shard_map/pallas_call | solution.py:616
  33.8 1.3 %copy.10 = f32[1,2,256,1024]{3,2,1,0:T(8,128)} copy(f32[1,2,256,1024]{3,2,1,0:T(8,128)S(1)} %bitcast.2) | data formatting | bytes 4194304

commit v4 on v3

--- a/solution.py
+++ b/solution.py
@@ -253,7 +253,6 @@
     barrier = pltpu.get_barrier_semaphore()
     early = region == 0
     late = region == count - 1
-    wraps = jnp.logical_or(early, late)
     for peer in ((other_cut, region), (c, steps[0].peer)):
         pl.semaphore_signal(barrier, 1, device_id=peer, device_id_type=pl.DeviceIdType.MESH)
 
@@ -277,7 +276,7 @@
 
     across = (other_cut, region)
     notes = [
-        [remote(scans[k], around[s][k], (c, steps[s].peer)) for k in range(2)] for s in range(2)
+        [remote(here[k], around[s][k], (c, steps[s].peer)) for k in range(2)] for s in range(2)
     ]
     near = [pl.ds(step.near_low, rim) for step in steps]
     far = [pl.ds(step.far_low, rim) for step in steps]
@@ -312,6 +311,8 @@
         remote(keep.at[s, :, far[s]], far_back.at[s, 0], (c, steps[s].peer)) for s in range(2)
     ]
     strip = [remote(strip_send.at[p], strip_in.at[p], (c, steps[1].peer)) for p in range(2)]
+    for load in loads[:2]:
+        load.wait()
     for note in notes[0]:
         note.start()
 
@@ -321,8 +322,7 @@
             note.start()
 
     with mark("band"):
-        for load in loads[:3]:
-            load.wait()
+        loads[2].wait()
 
     ids = lax.broadcasted_iota(jnp.int32, (rim, side), 0)
 
@@ -339,7 +339,7 @@
         rows = ids + (row + step.far_low)
         outside = jnp.logical_or(rows < 0, rows >= band_rows)
         if s == 1:
-            outside = jnp.logical_and(outside, jnp.logical_not(wraps))
+            outside = jnp.logical_and(outside, jnp.logical_not(early))
         return jnp.where(outside, far_in[s, j, plane].astype(jnp.float32), held)
 
     def near_half(s, rank, plane):
@@ -372,11 +372,10 @@
             own[s, plane, near[s]] = near_half(s, c, plane)
             own[s, plane, far[s]] = mixed(s, c, 1, plane)
 
-    def send_strip():
+    def send_strip(plane):
         rows = pl.ds(pl.multiple_of(rim + steps[1].peer_upper * (band_rows - rim), rim), rim)
-        for plane in range(2):
-            strip_send[plane] = ext[plane, rows].astype(jnp.bfloat16)
-            strip[plane].start()
+        strip_send[plane] = ext[plane, rows].astype(jnp.bfloat16)
+        strip[plane].start()
 
     def add_near(s, rank, source):
         step = steps[s]
@@ -441,22 +440,17 @@
         cut_near(0)
         x_near[0].start()
 
-    @pl.when(late)
-    def _():
-        send_strip()
-
     with mark("wnote"):
         for note in notes[0]:
             note.wait_recv()
-    for j in range(2):
-        cut_halo(0, j)
-        halo[0][j].start()
-    with mark("wh0"):
-        halo[0][0].wait_recv()
-    for plane in range(2):
-        send_far(0, plane)
-
-    @pl.when(jnp.logical_not(wraps))
+    cut_halo(0, 0)
+    halo[0][0].start()
+
+    @pl.when(late)
+    def _():
+        send_strip(0)
+
+    @pl.when(jnp.logical_not(jnp.logical_or(early, late)))
     def _():
         with mark("wnote"):
             for note in notes[1]:
@@ -464,6 +458,12 @@
         cut_halo(1, 0)
         halo[1][0].start()
 
+    with mark("wh0"):
+        halo[0][0].wait_recv()
+    for plane in range(2):
+        send_far(0, plane)
+    cut_halo(0, 1)
+    halo[0][1].start()
     with mark("prep"):
         cut_near(1)
         for load in loads[3:]:
@@ -471,6 +471,11 @@
         wave[0], wave[1] = turn(
             even_first(lambda first, k: phase[k, pl.ds(first, rim, stride=2), :])
         )
+
+        @pl.when(late)
+        def _():
+            send_strip(1)
+
         halo[0][1].wait_recv()
         gather_own(0)
         for s in range(2):
@@ -488,53 +493,70 @@
         with mark("wnote"):
             for note in notes[1]:
                 note.wait_recv()
-        send_strip()
+        cut_halo(1, 0)
+        halo[1][0].start()
         for note in notes[1]:
             note.start()
 
     with mark("wsA"):
-        for copy in [x_near[0]] + x_far[0]:
-            copy.wait_send()
+        x_near[0].wait_send()
+        x_far[0][0].wait_send()
     x_near[1].start()
 
-    @pl.when(jnp.logical_not(wraps))
+    @pl.when(jnp.logical_not(early))
+    def _():
+        with mark("wh1"):
+            halo[1][0].wait_recv()
+        for plane in range(2):
+            send_far(1, plane)
+
+    @pl.when(jnp.logical_not(late))
     def _():
         cut_halo(1, 1)
         halo[1][1].start()
-        with mark("wh1"):
-            halo[1][0].wait_recv()
-        for plane in range(2):
-            send_far(1, plane)
-
-    @pl.when(wraps)
-    def _():
-        send_strip_far(0)
 
     position_of(0)
-
-    @pl.when(wraps)
-    def _():
-        send_strip_far(1)
-
     back_own[0].start()
 
-    @pl.when(jnp.logical_not(wraps))
+    @pl.when(early)
+    def _():
+        for plane in range(2):
+            send_strip_far(plane)
+
+    give_parts[0][0].start()
+
+    @pl.when(early)
+    def _():
+        give_parts[0][1].start()
+        gather_own(1)
+
+    with mark("wsB"):
+        for copy in [x_far[0][1], x_near[1]] + x_far[1]:
+            copy.wait_send()
+
+    @pl.when(jnp.logical_not(early))
+    def _():
+        give_parts[0][1].start()
+
+    give_parts[0][2].start()
+
+    @pl.when(jnp.logical_not(early))
     def _():
         with mark("wh1"):
             halo[1][1].wait_recv()
-
-    with mark("own1"):
         gather_own(1)
+
     with mark("add"):
         add_near(0, c, keep)
-    with mark("wsB"):
-        for copy in [x_near[1]] + x_far[1]:
-            copy.wait_send()
-    for copy in give_parts[0]:
-        copy.start()
     position_of(1)
     for copy in give_parts[1][:2]:
         copy.start()
+
+    @pl.when(early)
+    def _():
+        for copy in give_parts[0][3:] + give_parts[1][2:]:
+            copy.start()
+
     back_own[1].start()
     with mark("wgf0"):
         for part, back in zip(give_parts[0], back_other[0]):
@@ -551,24 +573,44 @@
             note.wait_recv()
 
     with mark("wsC"):
-        give_parts[1][0].wait_send()
-    for copy in give_parts[1][2:]:
-        copy.start()
+        for copy in give_parts[0][:3] + give_parts[1][:2]:
+            copy.wait_send()
+
+    @pl.when(jnp.logical_not(early))
+    def _():
+        for copy in give_parts[0][3:] + give_parts[1][2:]:
+            copy.start()
+
+    @pl.when(late)
+    def _():
+        for copy in strip:
+            copy.wait_send()
+
+    @pl.when(jnp.logical_not(late))
+    def _():
+        for copy in halo[1]:
+            copy.wait_send()
+
+    for copy in notes[0] + notes[1] + halo[0] + [back_own[0]]:
+        copy.wait_send()
     with mark("wgf1"):
         for part, back in zip(give_parts[1], back_other[1]):
             part.wait_recv()
             back.start()
     with mark("add"):
-        for copy in give_parts[0][2:]:
-            copy.wait_recv()
-        add_near(0, other_cut, give_in)
-    with mark("add"):
         for copy in back_other[0]:
             copy.wait_recv()
         add_far(0, 1)
     with mark("add"):
         back_own[1].wait_recv()
         add_far(1, 0)
+    for copy in [back_own[1]] + back_other[0]:
+        copy.wait_send()
+    with mark("wgn0"):
+        for copy in give_parts[0][2:]:
+            copy.wait_recv()
+    with mark("add"):
+        add_near(0, other_cut, give_in)
     with mark("wgn"):
         give_parts[1][2].wait_recv()
     with mark("add"):
@@ -577,26 +619,13 @@
         give_parts[1][3].wait_recv()
     with mark("add"):
         add_end(1, other_cut, give_in)
+    for copy in give_parts[0][3:] + give_parts[1][2:] + back_other[1]:
+        copy.wait_send()
     with mark("wend"):
         for copy in back_other[1]:
             copy.wait_recv()
     with mark("add"):
         add_far(1, 1)
-
-    @pl.when(wraps)
-    def _():
-        for copy in strip:
-            copy.wait_send()
-
-    @pl.when(jnp.logical_not(wraps))
-    def _():
-        for copy in halo[1]:
-            copy.wait_send()
-
-    for copy in notes[0] + notes[1] + halo[0] + give_parts[0] + give_parts[1][1:]:
-        copy.wait_send()
-    for copy in back_own + back_other[0] + back_other[1]:
-        copy.wait_send()
 
 
 def shards(objects, probes, amplitudes, prop_phase, scan_rows, scan_cols, probe_choice):

time: 35.2 us -> 32.4 us (0.920)
  Pallas kernels: 33.8 us -> 30.9 us
    pallas_call x1, Pallas kernels: 33.8 us -> 30.9 us  [shards(): pl.pallas_call(functools.partial(wave_kernel, side, count), out_shape=jax...]
where the time goes in v4:
time: 32.4 us; the launch traced here: 32.2 us
  Pallas kernels  30.9 us (95%)
  local copies, waits for them, and re-layouts  1.32 us (4%)
    pallas_call x1, Pallas kernels, shards(): pl.pallas_call(functools.partial(wave_kernel, side, count), out_shape=jax...  30.9 us
    unnamed x1, local copies, waits for them, and re-layouts  1.32 us

profile of v4, /device:TPU:0, one launch (start us, length us, event | category | flops | bytes accessed | tf_op | source)
XLA Modules:
  0.0 32.2 jit_solution(321757257138986863)
XLA Ops:
  0.0 30.9 %shard_map.82 = f32[2,256,1024]{2,1,0:T(8,128)S(1)} custom-call(s32[4]{0:T(128)} %scans_0_.1, s32[4]{0:T(128)} %scans_1_.1, s32[4]{0:T(128)} %choice_any.1, f32[2,256,1024]{2,1,0:T(8,128)} %bitcast.3, bf16[4,2,256,256]{3,2,1,0:T(8,128)(2,1)} %probes_any.1, f32[4,256,256]{2,1,0:T(8,128)} %amps_any.1, f32[256,256]{1,0:T(8,128)} %phase_any.1, ...), custom_call_target="tpu_custom_call" | custom-call | tf_op jit(solution)/shard_map/pallas_call | solution.py:645
  30.9 1.3 %copy.10 = f32[1,2,256,1024]{3,2,1,0:T(8,128)} copy(f32[1,2,256,1024]{3,2,1,0:T(8,128)S(1)} %bitcast.2) | data formatting | bytes 4194304

commit v5 on v4

--- a/solution.py
+++ b/solution.py
@@ -238,17 +238,22 @@
     region = lax.axis_index("region")
     other_cut = 1 - c
     steps = [Step(s, region, count, side, band_rows) for s in range(2)]
+    cuts = [(p, k * rim) for p in range(2) for k in range(band_rows // rim)]
+    loads = [(scans[0], here[0]), (scans[1], here[1])]
+    loads += [
+        (band.at[p, pl.ds(low, rim)], ext.at[p, pl.ds(rim + low, rim)]) for p, low in cuts
+    ]
+    early_loads = len(loads)
+    loads += [
+        (choice_any, choice), (tables_any, tables), (probes_any, probes),
+        *((phase_any.at[:, pl.ds(k * rim, rim)], phase.at[k]) for k in range(2)),
+        *((amps_any.at[:, :, pl.ds(k * rim, rim)], amps.at[k]) for k in range(2)),
+    ]
     loads = [
-        pltpu.make_async_copy(source, target, local_sem.at[k])
-        for k, (source, target) in enumerate((
-            (scans[0], here[0]), (scans[1], here[1]),
-            (band, ext.at[:, pl.ds(rim, band_rows)]), (choice_any, choice),
-            (tables_any, tables), (probes_any, probes),
-            *((phase_any.at[:, pl.ds(k * rim, rim)], phase.at[k]) for k in range(2)),
-            *((amps_any.at[:, :, pl.ds(k * rim, rim)], amps.at[k]) for k in range(2)),
-        ))
+        pltpu.make_async_copy(source, target, local_sem.at[k % early_loads if k < 2 * early_loads else k - early_loads])
+        for k, (source, target) in enumerate(loads)
     ]
-    for load in loads:
+    for load in loads[:early_loads]:
         load.start()
     barrier = pltpu.get_barrier_semaphore()
     early = region == 0
@@ -264,53 +269,57 @@
 
     with mark("bar"):
         pl.semaphore_wait(barrier, jnp.where(early, 2, 3))
-    slots = iter(range(40))
-
-    def remote(source, target, peer):
-        slot = next(slots)
+    slots = iter(range(32))
+
+    def remote(source, target, peer, send_slot, recv_slot=None):
+        slot = next(slots) if recv_slot is None else recv_slot
         return pltpu.make_async_remote_copy(
             src_ref=source, dst_ref=target,
-            send_sem=send_sem.at[slot], recv_sem=recv_sem.at[slot],
+            send_sem=send_sem.at[send_slot], recv_sem=recv_sem.at[slot],
             device_id=peer, device_id_type=pl.DeviceIdType.MESH,
         )
 
     across = (other_cut, region)
-    notes = [
-        [remote(here[k], around[s][k], (c, steps[s].peer)) for k in range(2)] for s in range(2)
-    ]
+    halves = [(c, step.peer) for step in steps]
+    notes = [[remote(here[k], around[s][k], halves[s], 2 * s + k) for k in range(2)] for s in range(2)]
     near = [pl.ds(step.near_low, rim) for step in steps]
     far = [pl.ds(step.far_low, rim) for step in steps]
-    x_near = [remote(x_send.at[s, :, near[s]], x_in.at[s, :, near[s]], across) for s in range(2)]
+    x_near = [remote(x_send.at[s, :, near[s]], x_in.at[s, :, near[s]], across, 4 + 3 * s) for s in range(2)]
     x_far = [
-        [remote(x_send.at[s, p, far[s]], x_in.at[s, p, far[s]], across) for p in range(2)]
+        [remote(x_send.at[s, p, far[s]], x_in.at[s, p, far[s]], across, 5 + 3 * s + p) for p in range(2)]
         for s in range(2)
     ]
-    halo = [
-        [remote(far_send.at[s, j], far_in.at[s, j], (c, steps[s].peer)) for j in range(2)]
-        for s in range(2)
+    halo = [[remote(far_send.at[0, j], far_in.at[0, j], halves[0], 10 + j) for j in range(2)]]
+    halo.append([remote(far_send.at[1, j], far_in.at[1, j], halves[1], 12 + j, 10 + j + 2) for j in range(2)])
+    strip = [remote(strip_send.at[p], strip_in.at[p], halves[1], 12 + p, 10 + p + 2) for p in range(2)]
+    slots = iter(range(14, 32))
+    quarter = side // 4
+    rows = []
+    for step in steps:
+        order = [3 - k + step.upper * (2 * k - 3) for k in range(4)]
+        rows.append([pl.ds(pl.multiple_of(k * quarter, quarter), quarter) for k in order])
+    give_parts = [
+        [
+            remote(give.at[0, :, part], give_in.at[0, :, part], across, slot)
+            for part, slot in ((far[0], 5), (rows[0][2], 4), (rows[0][3], 6))
+        ],
+        [
+            remote(give.at[1, :, part], give_in.at[1, :, part], across, slot)
+            for part, slot in zip(rows[1], (7, 8, 9, 14))
+        ],
     ]
-    quarter = side // 4
-    give_parts, back_other = [], []
-    for s, step in enumerate(steps):
-        order = [3 - k + step.upper * (2 * k - 3) for k in range(4)]
-        rows = [pl.ds(pl.multiple_of(k * quarter, quarter), quarter) for k in order]
-        give_parts.append(
-            [remote(give.at[s, :, part], give_in.at[s, :, part], across) for part in rows]
+    back_other = [[remote(give_in.at[0, :, far[0]], far_back.at[0, 1], halves[0], 0)], []]
+    for k in range(2):
+        start = pl.multiple_of(jnp.where(steps[1].upper == 1, k, 1 - k) * quarter, quarter)
+        back_other[1].append(
+            remote(
+                give_in.at[1, :, rows[1][k]],
+                far_back.at[1, 1, :, pl.ds(start, quarter)],
+                halves[1],
+                1 + k,
+            )
         )
-        back_other.append([])
-        for part, k in zip(rows[:2], order[:2]):
-            start = pl.multiple_of(k * quarter - step.far_low, quarter)
-            back_other[s].append(
-                remote(
-                    give_in.at[s, :, part],
-                    far_back.at[s, 1, :, pl.ds(start, quarter)],
-                    (c, step.peer),
-                )
-            )
-    back_own = [
-        remote(keep.at[s, :, far[s]], far_back.at[s, 0], (c, steps[s].peer)) for s in range(2)
-    ]
-    strip = [remote(strip_send.at[p], strip_in.at[p], (c, steps[1].peer)) for p in range(2)]
+    back_own = [remote(keep.at[s, :, far[s]], far_back.at[s, 0], halves[s], 10 + s) for s in range(2)]
     for load in loads[:2]:
         load.wait()
     for note in notes[0]:
@@ -322,7 +331,10 @@
             note.start()
 
     with mark("band"):
-        loads[2].wait()
+        for load in loads[2:early_loads]:
+            load.wait()
+    for load in loads[early_loads:]:
+        load.start()
 
     ids = lax.broadcasted_iota(jnp.int32, (rim, side), 0)
 
@@ -388,13 +400,13 @@
             lay_window(near_laid, plane, row + low, place, part)
             add_laid(total, near_laid, plane, row + low, place, first, side - quarter, side)
 
-    def add_far(s, j):
+    def add_far(s, j, planes=(0, 1)):
         step = steps[s]
         row, col = corner(around[s], step.peer_upper, (c, other_cut)[j], side, band_rows)
         top = row + step.peer_offset + step.peer_far_low
         first = pl.multiple_of(step.peer_upper * rim, rim)
         place = split_col(col, total.shape[2], side)
-        for plane in range(2):
+        for plane in planes:
             part = far_back[s, j, plane].astype(jnp.float32)
             lay_window(far_laid, plane, top, place, part)
             add_laid(total, far_laid, plane, top, place, first, rim, side)
@@ -409,12 +421,12 @@
             lay_window(far_laid, plane, row + quarter, place, part)
             add_laid(total, far_laid, plane, row + quarter, place, first, rim, side)
 
-    def add_end(s, rank, source):
+    def add_end(s, rank, source, planes=(0, 1)):
         step = steps[s]
         row, col = corner(here, step.upper, rank, side, band_rows)
         low = pl.multiple_of(step.upper * 3 * quarter, quarter)
         place = split_col(col, total.shape[2], side)
-        for plane in range(2):
+        for plane in planes:
             part = source[s, plane, pl.ds(low, quarter)].astype(jnp.float32)
             lay_window(end_laid, plane, row + low, place, part)
             add_laid(total, end_laid, plane, row + low, place, quarter, rim, side)
@@ -466,7 +478,7 @@
     halo[0][1].start()
     with mark("prep"):
         cut_near(1)
-        for load in loads[3:]:
+        for load in loads[early_loads:]:
             load.wait()
         wave[0], wave[1] = turn(
             even_first(lambda first, k: phase[k, pl.ds(first, rim, stride=2), :])
@@ -515,6 +527,8 @@
         cut_halo(1, 1)
         halo[1][1].start()
 
+    for copy in notes[0] + notes[1] + halo[0]:
+        copy.wait_send()
     position_of(0)
     back_own[0].start()
 
@@ -523,11 +537,11 @@
         for plane in range(2):
             send_strip_far(plane)
 
-    give_parts[0][0].start()
+    give_parts[0][1].start()
 
     @pl.when(early)
     def _():
-        give_parts[0][1].start()
+        give_parts[0][0].start()
         gather_own(1)
 
     with mark("wsB"):
@@ -536,12 +550,7 @@
 
     @pl.when(jnp.logical_not(early))
     def _():
-        give_parts[0][1].start()
-
-    give_parts[0][2].start()
-
-    @pl.when(jnp.logical_not(early))
-    def _():
+        give_parts[0][0].start()
         with mark("wh1"):
             halo[1][1].wait_recv()
         gather_own(1)
@@ -554,7 +563,7 @@
 
     @pl.when(early)
     def _():
-        for copy in give_parts[0][3:] + give_parts[1][2:]:
+        for copy in give_parts[0][2:] + give_parts[1][2:]:
             copy.start()
 
     back_own[1].start()
@@ -573,12 +582,12 @@
             note.wait_recv()
 
     with mark("wsC"):
-        for copy in give_parts[0][:3] + give_parts[1][:2]:
+        for copy in give_parts[0][:2] + give_parts[1][:2]:
             copy.wait_send()
 
     @pl.when(jnp.logical_not(early))
     def _():
-        for copy in give_parts[0][3:] + give_parts[1][2:]:
+        for copy in give_parts[0][2:] + give_parts[1][2:]:
             copy.start()
 
     @pl.when(late)
@@ -591,8 +600,7 @@
         for copy in halo[1]:
             copy.wait_send()
 
-    for copy in notes[0] + notes[1] + halo[0] + [back_own[0]]:
-        copy.wait_send()
+    back_own[0].wait_send()
     with mark("wgf1"):
         for part, back in zip(give_parts[1], back_other[1]):
             part.wait_recv()
@@ -607,7 +615,7 @@
     for copy in [back_own[1]] + back_other[0]:
         copy.wait_send()
     with mark("wgn0"):
-        for copy in give_parts[0][2:]:
+        for copy in give_parts[0][1:]:
             copy.wait_recv()
     with mark("add"):
         add_near(0, other_cut, give_in)
@@ -615,17 +623,33 @@
         give_parts[1][2].wait_recv()
     with mark("add"):
         add_middle(1, other_cut, give_in)
-    with mark("wgn"):
-        give_parts[1][3].wait_recv()
-    with mark("add"):
+    for copy in give_parts[0][2:] + give_parts[1][2:]:
+        copy.wait_send()
+
+    def last_rows():
+        with mark("wgn"):
+            give_parts[1][3].wait_recv()
         add_end(1, other_cut, give_in)
-    for copy in give_parts[0][3:] + give_parts[1][2:] + back_other[1]:
+
+    def last_peer_rows():
+        with mark("wend"):
+            for copy in back_other[1]:
+                copy.wait_recv()
+        add_far(1, 1)
+
+    for copy in back_other[1]:
         copy.wait_send()
-    with mark("wend"):
-        for copy in back_other[1]:
-            copy.wait_recv()
-    with mark("add"):
-        add_far(1, 1)
+    order = (last_peer_rows, last_rows)
+
+    @pl.when(steps[1].upper == 1)
+    def _():
+        for part in order:
+            part()
+
+    @pl.when(steps[1].upper == 0)
+    def _():
+        for part in order[::-1]:
+            part()
 
 
 def shards(objects, probes, amplitudes, prop_phase, scan_rows, scan_cols, probe_choice):
@@ -660,9 +684,9 @@
             slot((2, rim, columns)), slot((2, rim, columns)),
             laid(side + side // 4), laid(side), laid(side - side // 4),
             (scalars,) * 2, ((scalars,) * 2,) * 2, scalars,
-            pltpu.SemaphoreType.DMA((10,)),
-            pltpu.SemaphoreType.DMA((40,)),
-            pltpu.SemaphoreType.DMA((40,)),
+            pltpu.SemaphoreType.DMA((7,)),
+            pltpu.SemaphoreType.DMA((15,)),
+            pltpu.SemaphoreType.DMA((26,)),
         ],
         compiler_params=pltpu.CompilerParams(
             collective_id=0, has_side_effects=True, vmem_limit_bytes=32 * 1024 * 1024

time: 32.4 us -> 31.9 us (0.985)
  Pallas kernels: 30.9 us -> 30.4 us
    pallas_call x1, Pallas kernels: 30.9 us -> 30.4 us  [shards(): pl.pallas_call(functools.partial(wave_kernel, side, count), out_shape=jax...]
where the time goes in v5:
time: 31.9 us; the launch traced here: 31.7 us
  Pallas kernels  30.4 us (95%)
  local copies, waits for them, and re-layouts  1.32 us (4%)
    pallas_call x1, Pallas kernels, shards(): pl.pallas_call(functools.partial(wave_kernel, side, count), out_shape=jax...  30.4 us
    unnamed x1, local copies, waits for them, and re-layouts  1.32 us

profile of v5, /device:TPU:0, one launch (start us, length us, event | category | flops | bytes accessed | tf_op | source)
XLA Modules:
  0.0 31.7 jit_solution(751402042959657686)
XLA Ops:
  0.0 30.4 %shard_map.82 = f32[2,256,1024]{2,1,0:T(8,128)S(1)} custom-call(s32[4]{0:T(128)} %scans_0_.1, s32[4]{0:T(128)} %scans_1_.1, s32[4]{0:T(128)} %choice_any.1, f32[2,256,1024]{2,1,0:T(8,128)} %bitcast.3, bf16[4,2,256,256]{3,2,1,0:T(8,128)(2,1)} %probes_any.1, f32[4,256,256]{2,1,0:T(8,128)} %amps_any.1, f32[256,256]{1,0:T(8,128)} %phase_any.1, ...), custom_call_target="tpu_custom_call" | custom-call | tf_op jit(solution)/shard_map/pallas_call | solution.py:669
  30.4 1.3 %copy.10 = f32[1,2,256,1024]{3,2,1,0:T(8,128)} copy(f32[1,2,256,1024]{3,2,1,0:T(8,128)S(1)} %bitcast.2) | data formatting | bytes 4194304

commit v6 on v5

--- a/solution.py
+++ b/solution.py
@@ -228,7 +228,7 @@
     side, count, scans, choice_any, band, probes_any, amps_any, phase_any, tables_any,
     total,
     ext, probes, amps, phase, wave, tables, measured,
-    x_send, x_in, far_send, far_in, own, give, keep, give_in, far_back, strip_send, strip_in,
+    x_send, x_in, far_send, far_in, own, give, keep, give_in, far_back, detour, strip_send, strip_in,
     near_laid, far_laid, end_laid, here, around, choice,
     local_sem, send_sem, recv_sem,
 ):
@@ -319,6 +319,8 @@
                 1 + k,
             )
         )
+    first_leg = remote(give.at[1, :, rows[1][0]], detour, halves[1], 7, 26)
+    second_leg = remote(detour, far_back.at[1, 1, :, pl.ds(0, quarter)], across, 15, 22)
     back_own = [remote(keep.at[s, :, far[s]], far_back.at[s, 0], halves[s], 10 + s) for s in range(2)]
     for load in loads[:2]:
         load.wait()
@@ -537,20 +539,26 @@
         for plane in range(2):
             send_strip_far(plane)
 
-    give_parts[0][1].start()
-
     @pl.when(early)
     def _():
-        give_parts[0][0].start()
         gather_own(1)
+
+    @pl.when(jnp.logical_not(early))
+    def _():
+        give_parts[0][1].start()
 
     with mark("wsB"):
         for copy in [x_far[0][1], x_near[1]] + x_far[1]:
             copy.wait_send()
+    give_parts[0][0].start()
+
+    @pl.when(early)
+    def _():
+        for copy in give_parts[0][1:]:
+            copy.start()
 
     @pl.when(jnp.logical_not(early))
     def _():
-        give_parts[0][0].start()
         with mark("wh1"):
             halo[1][1].wait_recv()
         gather_own(1)
@@ -558,10 +566,22 @@
     with mark("add"):
         add_near(0, c, keep)
     position_of(1)
-    for copy in give_parts[1][:2]:
-        copy.start()
-
     @pl.when(early)
+    def _():
+        first_leg.start()
+
+    @pl.when(jnp.logical_not(early))
+    def _():
+        give_parts[1][0].start()
+
+    give_parts[1][1].start()
+
+    @pl.when(early)
+    def _():
+        for copy in give_parts[1][2:]:
+            copy.start()
+
+    @pl.when(region == 1)
     def _():
         for copy in give_parts[0][2:] + give_parts[1][2:]:
             copy.start()
@@ -585,7 +605,7 @@
         for copy in give_parts[0][:2] + give_parts[1][:2]:
             copy.wait_send()
 
-    @pl.when(jnp.logical_not(early))
+    @pl.when(region > 1)
     def _():
         for copy in give_parts[0][2:] + give_parts[1][2:]:
             copy.start()
@@ -602,9 +622,15 @@
 
     back_own[0].wait_send()
     with mark("wgf1"):
-        for part, back in zip(give_parts[1], back_other[1]):
-            part.wait_recv()
-            back.start()
+
+        @pl.when(jnp.logical_not(early))
+        def _():
+            give_parts[1][0].wait_recv()
+            back_other[1][0].start()
+
+        give_parts[1][1].wait_recv()
+        back_other[1][1].start()
+
     with mark("add"):
         for copy in back_other[0]:
             copy.wait_recv()
@@ -619,13 +645,15 @@
             copy.wait_recv()
     with mark("add"):
         add_near(0, other_cut, give_in)
+    @pl.when(late)
+    def _():
+        first_leg.wait_recv()
+        second_leg.start()
+
     with mark("wgn"):
         give_parts[1][2].wait_recv()
     with mark("add"):
         add_middle(1, other_cut, give_in)
-    for copy in give_parts[0][2:] + give_parts[1][2:]:
-        copy.wait_send()
-
     def last_rows():
         with mark("wgn"):
             give_parts[1][3].wait_recv()
@@ -637,19 +665,30 @@
                 copy.wait_recv()
         add_far(1, 1)
 
-    for copy in back_other[1]:
-        copy.wait_send()
     order = (last_peer_rows, last_rows)
 
-    @pl.when(steps[1].upper == 1)
+    peer_first = jnp.logical_and(steps[1].upper == 1, jnp.logical_not(early))
+
+    @pl.when(peer_first)
     def _():
         for part in order:
             part()
 
-    @pl.when(steps[1].upper == 0)
+    @pl.when(jnp.logical_not(peer_first))
     def _():
         for part in order[::-1]:
             part()
+
+    for copy in give_parts[0][2:] + give_parts[1][2:] + back_other[1][1:]:
+        copy.wait_send()
+
+    @pl.when(jnp.logical_not(early))
+    def _():
+        back_other[1][0].wait_send()
+
+    @pl.when(late)
+    def _():
+        second_leg.wait_send()
 
 
 def shards(objects, probes, amplitudes, prop_phase, scan_rows, scan_cols, probe_choice):
@@ -681,12 +720,12 @@
             pltpu.VMEM((2, side, side), jnp.float32),
             slot(whole), slot(whole), slot(half), slot(half),
             pltpu.VMEM(whole, jnp.float32), slot(whole), slot(whole), slot(whole), slot(half),
-            slot((2, rim, columns)), slot((2, rim, columns)),
+            slot((2, side // 4, side)), slot((2, rim, columns)), slot((2, rim, columns)),
             laid(side + side // 4), laid(side), laid(side - side // 4),
             (scalars,) * 2, ((scalars,) * 2,) * 2, scalars,
             pltpu.SemaphoreType.DMA((7,)),
-            pltpu.SemaphoreType.DMA((15,)),
-            pltpu.SemaphoreType.DMA((26,)),
+            pltpu.SemaphoreType.DMA((16,)),
+            pltpu.SemaphoreType.DMA((27,)),
         ],
         compiler_params=pltpu.CompilerParams(
             collective_id=0, has_side_effects=True, vmem_limit_bytes=32 * 1024 * 1024

time: 31.9 us -> 31.7 us (level)
  no operation moved by 1% of the time
where the time goes in v6:
time: 31.7 us; the launch traced here: 31.5 us
  Pallas kernels  30.2 us (95%)
  local copies, waits for them, and re-layouts  1.32 us (4%)
    pallas_call x1, Pallas kernels, shards(): pl.pallas_call(functools.partial(wave_kernel, side, count), out_shape=jax...  30.2 us
    unnamed x1, local copies, waits for them, and re-layouts  1.32 us

profile of v6, /device:TPU:0, one launch (start us, length us, event | category | flops | bytes accessed | tf_op | source)
XLA Modules:
  0.0 31.5 jit_solution(10218205053360748027)
XLA Ops:
  0.0 30.2 %shard_map.82 = f32[2,256,1024]{2,1,0:T(8,128)S(1)} custom-call(s32[4]{0:T(128)} %scans_0_.1, s32[4]{0:T(128)} %scans_1_.1, s32[4]{0:T(128)} %choice_any.1, f32[2,256,1024]{2,1,0:T(8,128)} %bitcast.3, bf16[4,2,256,256]{3,2,1,0:T(8,128)(2,1)} %probes_any.1, f32[4,256,256]{2,1,0:T(8,128)} %amps_any.1, f32[256,256]{1,0:T(8,128)} %phase_any.1, ...), custom_call_target="tpu_custom_call" | custom-call | tf_op jit(solution)/shard_map/pallas_call | solution.py:708
  30.2 1.3 %copy.10 = f32[1,2,256,1024]{3,2,1,0:T(8,128)} copy(f32[1,2,256,1024]{3,2,1,0:T(8,128)S(1)} %bitcast.2) | data formatting | bytes 4194304

commit v7 on v6

--- a/solution.py
+++ b/solution.py
@@ -319,8 +319,9 @@
                 1 + k,
             )
         )
+    begin = pl.multiple_of(steps[1].upper * quarter, quarter)
     first_leg = remote(give.at[1, :, rows[1][0]], detour, halves[1], 7, 26)
-    second_leg = remote(detour, far_back.at[1, 1, :, pl.ds(0, quarter)], across, 15, 22)
+    second_leg = remote(detour, far_back.at[1, 1, :, pl.ds(begin, quarter)], across, 15, 22)
     back_own = [remote(keep.at[s, :, far[s]], far_back.at[s, 0], halves[s], 10 + s) for s in range(2)]
     for load in loads[:2]:
         load.wait()
@@ -550,7 +551,10 @@
     with mark("wsB"):
         for copy in [x_far[0][1], x_near[1]] + x_far[1]:
             copy.wait_send()
-    give_parts[0][0].start()
+
+    @pl.when(jnp.logical_not(late))
+    def _():
+        give_parts[0][0].start()
 
     @pl.when(early)
     def _():
@@ -566,11 +570,11 @@
     with mark("add"):
         add_near(0, c, keep)
     position_of(1)
-    @pl.when(early)
+    @pl.when(region < 2)
     def _():
         first_leg.start()
 
-    @pl.when(jnp.logical_not(early))
+    @pl.when(region >= 2)
     def _():
         give_parts[1][0].start()
 
@@ -587,10 +591,15 @@
             copy.start()
 
     back_own[1].start()
-    with mark("wgf0"):
-        for part, back in zip(give_parts[0], back_other[0]):
-            part.wait_recv()
-            back.start()
+    def pass_first():
+        with mark("wgf0"):
+            give_parts[0][0].wait_recv()
+        back_other[0][0].start()
+
+    @pl.when(jnp.logical_not(late))
+    def _():
+        pass_first()
+
     with mark("add"):
         back_own[0].wait_recv()
         add_far(0, 0)
@@ -602,8 +611,13 @@
             note.wait_recv()
 
     with mark("wsC"):
-        for copy in give_parts[0][:2] + give_parts[1][:2]:
+        for copy in give_parts[0][1:2] + give_parts[1][:2]:
             copy.wait_send()
+
+    @pl.when(late)
+    def _():
+        give_parts[0][0].start()
+
 
     @pl.when(region > 1)
     def _():
@@ -623,13 +637,24 @@
     back_own[0].wait_send()
     with mark("wgf1"):
 
-        @pl.when(jnp.logical_not(early))
+        @pl.when(region >= 2)
         def _():
             give_parts[1][0].wait_recv()
             back_other[1][0].start()
 
         give_parts[1][1].wait_recv()
         back_other[1][1].start()
+
+    passes_on = jnp.logical_or(late, region == 2)
+
+    @pl.when(region == 2)
+    def _():
+        first_leg.wait_recv()
+        second_leg.start()
+
+    @pl.when(late)
+    def _():
+        pass_first()
 
     with mark("add"):
         for copy in back_other[0]:
@@ -679,14 +704,14 @@
         for part in order[::-1]:
             part()
 
-    for copy in give_parts[0][2:] + give_parts[1][2:] + back_other[1][1:]:
+    for copy in give_parts[0][:1] + give_parts[0][2:] + give_parts[1][2:] + back_other[1][1:]:
         copy.wait_send()
 
-    @pl.when(jnp.logical_not(early))
+    @pl.when(region >= 2)
     def _():
         back_other[1][0].wait_send()
 
-    @pl.when(late)
+    @pl.when(passes_on)
     def _():
         second_leg.wait_send()
 

time: 31.7 us -> 31.2 us (0.984)
  Pallas kernels: 30.2 us -> 29.7 us
    pallas_call x1, Pallas kernels: 30.2 us -> 29.7 us  [shards(): pl.pallas_call(functools.partial(wave_kernel, side, count), out_shape=jax...]
where the time goes in v7:
time: 31.2 us; the launch traced here: 31 us
  Pallas kernels  29.7 us (95%)
  local copies, waits for them, and re-layouts  1.32 us (4%)
    pallas_call x1, Pallas kernels, shards(): pl.pallas_call(functools.partial(wave_kernel, side, count), out_shape=jax...  29.7 us
    unnamed x1, local copies, waits for them, and re-layouts  1.32 us

profile of v7, /device:TPU:0, one launch (start us, length us, event | category | flops | bytes accessed | tf_op | source)
XLA Modules:
  0.0 31.0 jit_solution(5635165536779759161)
XLA Ops:
  0.0 29.7 %shard_map.82 = f32[2,256,1024]{2,1,0:T(8,128)S(1)} custom-call(s32[4]{0:T(128)} %scans_0_.1, s32[4]{0:T(128)} %scans_1_.1, s32[4]{0:T(128)} %choice_any.1, f32[2,256,1024]{2,1,0:T(8,128)} %bitcast.3, bf16[4,2,256,256]{3,2,1,0:T(8,128)(2,1)} %probes_any.1, f32[4,256,256]{2,1,0:T(8,128)} %amps_any.1, f32[256,256]{1,0:T(8,128)} %phase_any.1, ...), custom_call_target="tpu_custom_call" | custom-call | tf_op jit(solution)/shard_map/pallas_call | solution.py:733
  29.7 1.3 %copy.10 = f32[1,2,256,1024]{3,2,1,0:T(8,128)} copy(f32[1,2,256,1024]{3,2,1,0:T(8,128)S(1)} %bitcast.2) | data formatting | bytes 4194304

commit v8 on v7

--- a/solution.py
+++ b/solution.py
@@ -574,11 +574,15 @@
     def _():
         first_leg.start()
 
-    @pl.when(region >= 2)
+    yields = region == count - 2
+
+    @pl.when(jnp.logical_and(region >= 2, jnp.logical_not(yields)))
     def _():
         give_parts[1][0].start()
 
-    give_parts[1][1].start()
+    @pl.when(jnp.logical_not(yields))
+    def _():
+        give_parts[1][1].start()
 
     @pl.when(early)
     def _():
@@ -604,6 +608,11 @@
         back_own[0].wait_recv()
         add_far(0, 0)
         add_near(1, c, keep)
+
+    @pl.when(yields)
+    def _():
+        for copy in give_parts[1][:2]:
+            copy.start()
 
     @pl.when(late)
     def _():

time: 31.2 us -> 31.1 us (level)
  the two profiles are of different devices: /device:TPU:0 before, /device:TPU:29 now
where the time goes in v8:
time: 31.1 us; the launch traced here: 31 us
  Pallas kernels  29.6 us (95%)
  local copies, waits for them, and re-layouts  1.32 us (4%)
    pallas_call x1, Pallas kernels, shards(): pl.pallas_call(functools.partial(wave_kernel, side, count), out_shape=jax...  29.6 us
    unnamed x1, local copies, waits for them, and re-layouts  1.32 us

profile of v8, /device:TPU:29, one launch (start us, length us, event | category | flops | bytes accessed | tf_op | source)
XLA Modules:
  0.0 31.0 jit_solution(1948499251919390907)
XLA Ops:
  0.0 29.6 %shard_map.82 = f32[2,256,1024]{2,1,0:T(8,128)S(1)} custom-call(s32[4]{0:T(128)} %scans_0_.1, s32[4]{0:T(128)} %scans_1_.1, s32[4]{0:T(128)} %choice_any.1, f32[2,256,1024]{2,1,0:T(8,128)} %bitcast.3, bf16[4,2,256,256]{3,2,1,0:T(8,128)(2,1)} %probes_any.1, f32[4,256,256]{2,1,0:T(8,128)} %amps_any.1, f32[256,256]{1,0:T(8,128)} %phase_any.1, ...), custom_call_target="tpu_custom_call" | custom-call | tf_op jit(solution)/shard_map/pallas_call | solution.py:742
  29.6 1.3 %copy.10 = f32[1,2,256,1024]{3,2,1,0:T(8,128)} copy(f32[1,2,256,1024]{3,2,1,0:T(8,128)S(1)} %bitcast.2) | data formatting | bytes 4194304
